TPU v7x, 256 devices: a whole 4x4x8 slice. The times are simulated.
256 devices in a mesh: band: 8 (over z_hi, core), dom: 32 (over y, x, z_lo).
Axes of the slice: x: 4, y: 4, z: 8 (z_hi: 4, z_lo: 2; z = z_hi * 2 + z_lo), core: 2. Of those that a mesh axis runs over, the one named last changes fastest.
Arguments:
- orbital_block: bfloat16 [8192, 4096], P('dom', 'band'), may hold values from -6 to 6
- cell_matrices: bfloat16 [128, 125, 125], P('dom'), may hold values from -0.09 to 0.09, as said below
- cell_nodes: int32 [125, 128], P(None, 'dom'), may hold values from 0 to 319, as said below
- shared_nodes: int32 [32, 64], P('dom'), may hold values from 0 to 255, as said below
- inv_sqrt_mass: float32 [8192], P('dom'), may hold values from 0.8 to 1.25
- potential: float32 [8192], P('dom'), may hold values from -0.5 to 0.3
- filter_center: float32 [1], replicated, may hold values from -0.1 to 0.1
- filter_halfwidth: float32 [1], replicated, may hold values from 0.8 to 1.2
Outputs:
- filtered: bfloat16 [8192, 4096], P('dom', 'band')
- intersection: float32 [4096, 4096], P(('band', 'dom'))
- projected: float32 [4096, 4096], P(('band', 'dom'))
Inputs may be any that keep to these rules, and one draw needn't show every extreme that they name: `cell_matrices`: each cell's matrix is symmetric. `cell_nodes`: column c lists the 125 nodes of cell c, a hexahedron of degree 4 with its nodes in lexicographic order, numbered as the device that holds the cell sees them: a value below 256 is one of its own nodes, a value 256 + j is entry j of the next device's (cyclically) shared list. Every own node and every shared entry is used by some cell. `shared_nodes`: row d holds 64 distinct own nodes of device d, which cells of device d - 1 (cyclically) also use.
All inputs are finite; a program needn't handle non-finite values.
Results may differ from a plain program's by a relative error of at most 0.024.
Values may be sent and summed in bfloat16 or wider, within the bound.
A program may use at most 64 MiB of HBM per device.

v0:
```python
import jax
import jax.numpy as jnp
from jax import lax
from jax.sharding import PartitionSpec as P

FILTER_DEG = 4


def shifted(block, axis, distance):
    devices = range(lax.axis_size(axis))
    route = [((i - distance) % len(devices), i) for i in devices]
    return lax.ppermute(block, axis, route)


def hamilton(field, cell_matrices, cell_nodes, shared_local, inv_mass, potential):
    scaled = (inv_mass[:, None] * field).astype(jnp.bfloat16)
    ghost_rows = shifted(scaled[shared_local], "dom", -1)
    extended = jnp.concatenate([scaled, ghost_rows], axis=0)
    gathered = extended[cell_nodes]
    cell_out = jnp.einsum(
        "cij,jck->ick", cell_matrices, gathered, preferred_element_type=jnp.float32
    )
    node_count = field.shape[0]
    columns = field.shape[1]
    summed = jnp.zeros((node_count + ghost_rows.shape[0], columns), jnp.float32)
    summed = summed.at[cell_nodes.reshape(-1)].add(cell_out.reshape(-1, columns))
    incoming = shifted(summed[node_count:], "dom", 1)
    assembled = summed[:node_count].at[shared_local].add(incoming)
    return inv_mass[:, None] * assembled + potential[:, None] * field


def contract(left, right):
    return lax.dot_general(
        left, right, (((0,), (0,)), ((), ())), preferred_element_type=jnp.float32
    )


def shards(
    orbital_block,
    cell_matrices,
    cell_nodes,
    shared_nodes,
    inv_sqrt_mass,
    potential,
    filter_center,
    filter_halfwidth,
):
    shared_local = shared_nodes[0]
    center = filter_center[0]
    halfwidth = filter_halfwidth[0]

    def apply_ham(field):
        return hamilton(field, cell_matrices, cell_nodes, shared_local, inv_sqrt_mass, potential)

    def mapped(field):
        return (apply_ham(field) - center * field) / halfwidth

    previous = orbital_block.astype(jnp.float32)
    current = mapped(previous)
    for degree_step in range(FILTER_DEG - 1):
        following = 2.0 * mapped(current) - previous
        previous = current
        current = following
    filtered = current.astype(jnp.bfloat16)
    applied = apply_ham(filtered.astype(jnp.float32)).astype(jnp.bfloat16)
    band_count = lax.axis_size("band")
    dom_count = lax.axis_size("dom")
    my_group = lax.axis_index("band")
    block_width = filtered.shape[1]
    all_columns = block_width * band_count
    factor = 1.0 / (filtered.shape[0] * dom_count)
    intersection = jnp.zeros((block_width, all_columns), jnp.float32)
    projected = jnp.zeros((block_width, all_columns), jnp.float32)
    moving = filtered
    moving_applied = applied
    for cycle_step in range(band_count):
        if cycle_step > 0:
            moving, moving_applied = shifted((moving, moving_applied), "band", 1)
        source_group = (my_group - cycle_step) % band_count
        piece_intersection = contract(filtered, moving)
        piece_projected = contract(filtered, moving_applied)
        column_start = source_group * block_width
        zero_row = jnp.zeros((), jnp.int32)
        intersection = lax.dynamic_update_slice(
            intersection, piece_intersection, (zero_row, column_start)
        )
        projected = lax.dynamic_update_slice(projected, piece_projected, (zero_row, column_start))
    intersection, projected = (
        lax.psum_scatter(
            intersection.astype(jnp.bfloat16), "dom", scatter_dimension=0, tiled=True
        ).astype(jnp.float32),
        lax.psum_scatter(
            projected.astype(jnp.bfloat16), "dom", scatter_dimension=0, tiled=True
        ).astype(jnp.float32),
    )
    return (filtered, intersection * factor, projected * factor)


def solution(mesh):
    return jax.shard_map(
        shards,
        mesh=mesh,
        in_specs=(
            P("dom", "band"),
            P("dom", None, None),
            P(None, "dom"),
            P("dom", None),
            P("dom"),
            P("dom"),
            P(),
            P(),
        ),
        out_specs=(P("dom", "band"), P(("band", "dom"), None), P(("band", "dom"), None)),
        check_vma=False,
    )
```

profile of v0, /device:TPU:2, one launch (start us, length us, event | category | flops | bytes accessed | tf_op | source)
XLA Modules:
  0.0 545.2 jit_solution(4070859678689547869)
XLA Ops:
  9.7 2.0 collective-permute-start
  14.1 2.1 gather_fusion.1
  17.8 3.7 scatter_custom_fusion
  21.5 2.9 collective-permute-start.1
  25.7 1.7 collective-permute-done.1
  27.5 1.2 scatter_fusion
  29.6 3.8 collective-permute-start.2
  33.4 1.9 collective-permute-done.2
  35.3 2.1 gather_fusion.3
  38.7 1.3 reshape.192
  40.0 4.3 scatter_custom_fusion.2
  44.3 1.7 collective-permute-start.3
  46.1 7.6 %collective-permute-done.3 = f32[64,512]{1,0:T(8,128)S(1)} collective-permute-done((f32[64,512]{1,0:T(8,128)S(1)}, f32[64,512]{1,0:T(8,128)S(1)}, u32[]{:S(2)}, u32[]{:S(2)}) %collective-permute-start.3) | collective-permute-done | bytes 131104 | tf_op jit(solution)/shard_map/ppermute | solution.py:12
  53.7 1.2 scatter_fusion.1
  56.0 2.8 collective-permute-start.4
  58.8 1.9 collective-permute-done.4
  60.8 2.1 gather_fusion.5
  64.1 1.3 reshape.208
  65.4 4.3 scatter_custom_fusion.4
  69.9 9.1 %collective-permute-done.5 = f32[64,512]{1,0:T(8,128)S(1)} collective-permute-done((f32[64,512]{1,0:T(8,128)S(1)}, f32[64,512]{1,0:T(8,128)S(1)}, u32[]{:S(2)}, u32[]{:S(2)}) %collective-permute-start.5) | collective-permute-done | bytes 131104 | tf_op jit(solution)/shard_map/ppermute | solution.py:12
  79.0 1.2 scatter_fusion.2
  81.3 3.0 collective-permute-start.6
  84.3 1.9 collective-permute-done.6
  86.2 2.1 gather_fusion.7
  89.6 1.3 reshape.224
  90.9 4.3 scatter_custom_fusion.6
  95.5 9.3 %collective-permute-done.7 = f32[64,512]{1,0:T(8,128)S(1)} collective-permute-done((f32[64,512]{1,0:T(8,128)S(1)}, f32[64,512]{1,0:T(8,128)S(1)}, u32[]{:S(2)}, u32[]{:S(2)}) %collective-permute-start.7) | collective-permute-done | bytes 131104 | tf_op jit(solution)/shard_map/ppermute | solution.py:12
  104.9 1.2 scatter_fusion.3
  106.4 2.4 broadcast.76.clone
  110.0 4.8 collective-permute-done.8
  116.0 7.7 %collective-permute-done.9 = bf16[256,512]{1,0:T(8,128)(2,1)S(1)} collective-permute-done((bf16[256,512]{1,0:T(8,128)(2,1)S(1)}, bf16[256,512]{1,0:T(8,128)(2,1)S(1)}, u32[]{:S(2)}, u32[]{:S(2)}) %collective-permute-start.9) | collective-permute-done | bytes 262176 | tf_op jit(solution)/shard_map/ppermute | solution.py:12
  123.6 1.2 convolution_dynamic-update-slice_fusion.13
  124.9 6.7 %collective-permute-done.10 = bf16[256,512]{1,0:T(8,128)(2,1)S(1)} collective-permute-done((bf16[256,512]{1,0:T(8,128)(2,1)S(1)}, bf16[256,512]{1,0:T(8,128)(2,1)S(1)}, u32[]{:S(2)}, u32[]{:S(2)}) %collective-permute-start.10) | collective-permute-done | bytes 262176 | tf_op jit(solution)/shard_map/ppermute | solution.py:12
  131.6 1.2 convolution_dynamic-update-slice_fusion.12
  132.8 6.8 %collective-permute-done.11 = bf16[256,512]{1,0:T(8,128)(2,1)S(1)} collective-permute-done((bf16[256,512]{1,0:T(8,128)(2,1)S(1)}, bf16[256,512]{1,0:T(8,128)(2,1)S(1)}, u32[]{:S(2)}, u32[]{:S(2)}) %collective-permute-start.11) | collective-permute-done | bytes 262176 | tf_op jit(solution)/shard_map/ppermute | solution.py:12
  139.6 1.2 convolution_dynamic-update-slice_fusion.11
  140.7 9.6 %collective-permute-done.12 = bf16[256,512]{1,0:T(8,128)(2,1)S(1)} collective-permute-done((bf16[256,512]{1,0:T(8,128)(2,1)S(1)}, bf16[256,512]{1,0:T(8,128)(2,1)S(1)}, u32[]{:S(2)}, u32[]{:S(2)}) %collective-permute-start.12) | collective-permute-done | bytes 262176 | tf_op jit(solution)/shard_map/ppermute | solution.py:12
  150.6 1.2 convolution_dynamic-update-slice_fusion.10
  151.8 7.7 %collective-permute-done.13 = bf16[256,512]{1,0:T(8,128)(2,1)S(1)} collective-permute-done((bf16[256,512]{1,0:T(8,128)(2,1)S(1)}, bf16[256,512]{1,0:T(8,128)(2,1)S(1)}, u32[]{:S(2)}, u32[]{:S(2)}) %collective-permute-start.13) | collective-permute-done | bytes 262176 | tf_op jit(solution)/shard_map/ppermute | solution.py:12
  160.6 6.7 %collective-permute-done.14 = bf16[256,512]{1,0:T(8,128)(2,1)S(1)} collective-permute-done((bf16[256,512]{1,0:T(8,128)(2,1)S(1)}, bf16[256,512]{1,0:T(8,128)(2,1)S(1)}, u32[]{:S(2)}, u32[]{:S(2)}) %collective-permute-start.14) | collective-permute-done | bytes 262176 | tf_op jit(solution)/shard_map/ppermute | solution.py:12
  169.3 2.8 collective-permute-start.15
  172.1 1.9 collective-permute-done.15
  174.0 2.1 gather_fusion.9
  177.7 3.7 scatter_custom_fusion.8
  181.5 11.3 %collective-permute-done.16 = f32[64,512]{1,0:T(8,128)S(1)} collective-permute-done((f32[64,512]{1,0:T(8,128)S(1)}, f32[64,512]{1,0:T(8,128)S(1)}, u32[]{:S(2)}, u32[]{:S(2)}) %collective-permute-start.16) | collective-permute-done | bytes 131104 | tf_op jit(solution)/shard_map/ppermute | solution.py:12
  192.8 1.2 scatter_fusion.4
  194.3 2.5 broadcast.76.clone.1
  196.7 1.2 convolution_dynamic-update-slice_fusion.7
  198.0 15.2 %collective-permute-done.17 = bf16[256,512]{1,0:T(8,128)(2,1)S(1)} collective-permute-done((bf16[256,512]{1,0:T(8,128)(2,1)S(1)}, bf16[256,512]{1,0:T(8,128)(2,1)S(1)}, u32[]{:S(2)}, u32[]{:S(2)}) %collective-permute-start.17) | collective-permute-done | bytes 262176 | tf_op jit(solution)/shard_map/ppermute | solution.py:12
  214.3 17.6 %collective-permute-done.18 = bf16[256,512]{1,0:T(8,128)(2,1)S(1)} collective-permute-done((bf16[256,512]{1,0:T(8,128)(2,1)S(1)}, bf16[256,512]{1,0:T(8,128)(2,1)S(1)}, u32[]{:S(2)}, u32[]{:S(2)}) %collective-permute-start.18) | collective-permute-done | bytes 262176 | tf_op jit(solution)/shard_map/ppermute | solution.py:12
  232.1 1.2 convolution_dynamic-update-slice_fusion.5
  233.3 13.6 %collective-permute-done.19 = bf16[256,512]{1,0:T(8,128)(2,1)S(1)} collective-permute-done((bf16[256,512]{1,0:T(8,128)(2,1)S(1)}, bf16[256,512]{1,0:T(8,128)(2,1)S(1)}, u32[]{:S(2)}, u32[]{:S(2)}) %collective-permute-start.19) | collective-permute-done | bytes 262176 | tf_op jit(solution)/shard_map/ppermute | solution.py:12
  248.1 9.0 %collective-permute-done.20 = bf16[256,512]{1,0:T(8,128)(2,1)S(1)} collective-permute-done((bf16[256,512]{1,0:T(8,128)(2,1)S(1)}, bf16[256,512]{1,0:T(8,128)(2,1)S(1)}, u32[]{:S(2)}, u32[]{:S(2)}) %collective-permute-start.20) | collective-permute-done | bytes 262176 | tf_op jit(solution)/shard_map/ppermute | solution.py:12
  257.1 1.2 convolution_dynamic-update-slice_fusion.3
  258.3 10.3 %collective-permute-done.21 = bf16[256,512]{1,0:T(8,128)(2,1)S(1)} collective-permute-done((bf16[256,512]{1,0:T(8,128)(2,1)S(1)}, bf16[256,512]{1,0:T(8,128)(2,1)S(1)}, u32[]{:S(2)}, u32[]{:S(2)}) %collective-permute-start.21) | collective-permute-done | bytes 262176 | tf_op jit(solution)/shard_map/ppermute | solution.py:12
  268.6 1.2 convolution_dynamic-update-slice_fusion.2
  269.8 10.5 %collective-permute-done.22 = bf16[256,512]{1,0:T(8,128)(2,1)S(1)} collective-permute-done((bf16[256,512]{1,0:T(8,128)(2,1)S(1)}, bf16[256,512]{1,0:T(8,128)(2,1)S(1)}, u32[]{:S(2)}, u32[]{:S(2)}) %collective-permute-start.22) | collective-permute-done | bytes 262176 | tf_op jit(solution)/shard_map/ppermute | solution.py:12
  280.3 1.2 convolution_dynamic-update-slice_fusion.1
  281.5 10.8 %collective-permute-done.23 = bf16[256,512]{1,0:T(8,128)(2,1)S(1)} collective-permute-done((bf16[256,512]{1,0:T(8,128)(2,1)S(1)}, bf16[256,512]{1,0:T(8,128)(2,1)S(1)}, u32[]{:S(2)}, u32[]{:S(2)}) %collective-permute-start.23) | collective-permute-done | bytes 262176 | tf_op jit(solution)/shard_map/ppermute | solution.py:12
  292.3 1.2 convolution_dynamic-update-slice_fusion
  293.5 62.8 %reduce-scatter.3.cloned.1.call-done = bf16[16,4096]{1,0:T(8,128)(2,1)} async-done(((bf16[512,4096]{1,0:T(8,128)(2,1)}), bf16[16,4096]{1,0:T(8,128)(2,1)}) %reduce-scatter.3.cloned.1.call-update) | async-done | bytes 131088 | tf_op jit(solution)/shard_map/reduce_scatter | solution.py:89
  356.3 1.6 convert_multiply_fusion.6
  358.0 178.4 %reduce-scatter.5.cloned.1.call-done = bf16[16,4096]{1,0:T(8,128)(2,1)} async-done(((bf16[512,4096]{1,0:T(8,128)(2,1)}), bf16[16,4096]{1,0:T(8,128)(2,1)}) %reduce-scatter.5.cloned.1.call-update) | async-done | bytes 131088 | tf_op jit(solution)/shard_map/reduce_scatter | solution.py:92
  536.3 1.6 convert_multiply_fusion.5
  (90 shorter events, 23.9 us)
Async XLA Ops:
  7.2 9.3 %copy-start = (bf16[4,125,125]{2,0,1:T(4,128)(2,1)S(1)}, bf16[4,125,125]{2,0,1:T(4,128)(2,1)}, u32[]{:S(2)}) copy-start(bf16[4,125,125]{2,0,1:T(4,128)(2,1)} %param.9) | copy-start | bytes 375004
  7.2 349.2 %reduce-scatter.3.cloned.1.call-start = ((), (), s32[]{:S(2)}) async-start(), calls=%async_computation.2 | async-start | bytes 4325376 | tf_op jit(solution)/shard_map/reduce_scatter | solution.py:89
  9.7 4.3 collective-permute-start
  16.7 11.9 %copy-start.2 = (bf16[256,512]{1,0:T(8,128)(2,1)S(1)}, bf16[256,512]{1,0:T(8,128)(2,1)}, u32[]{:S(2)}) copy-start(bf16[256,512]{1,0:T(8,128)(2,1)} %param.8) | copy-start | bytes 786436
  16.8 11.9 %copy-start.3 = (f32[256]{0:T(256)S(1)}, f32[256]{0:T(256)}, u32[]{:S(2)}) copy-start(f32[256]{0:T(256)} %param.12) | copy-start | bytes 3076
  16.8 11.9 %copy-start.4 = (f32[256]{0:T(256)S(1)}, f32[256]{0:T(256)}, u32[]{:S(2)}) copy-start(f32[256]{0:T(256)} %param.13) | copy-start | bytes 3076
  21.5 5.9 %collective-permute-start.1 = (f32[64,512]{1,0:T(8,128)S(1)}, f32[64,512]{1,0:T(8,128)S(1)}, u32[]{:S(2)}, u32[]{:S(2)}) collective-permute-start(f32[64,512]{1,0:T(8,128)S(1)} %slice.61), channel_id=1, source_target_pairs={{31,0},{0,1},{1,2},{2,3},{3,4},{4,5},{5,6},{6,7},{7,8},{8,9},{9,10... | collective-permute-start | bytes 393224 | tf_op jit(solution)/shard_map/ppermute | solution.py:12
  29.6 5.7 %collective-permute-start.2 = (bf16[64,512]{1,0:T(8,128)(2,1)S(1)}, bf16[64,512]{1,0:T(8,128)(2,1)S(1)}, u32[]{:S(2)}, u32[]{:S(2)}) collective-permute-start(bf16[64,512]{1,0:T(8,128)(2,1)S(1)} %gather_fusion.2), channel_id=1, source_target_pairs={{1,0},{2,1},{3,2},{4,3},{5,4},{6,5},{7,6},{8,7},{9,8},{10,9},{11,1... | collective-permute-start | bytes 196616 | tf_op jit(solution)/shard_map/ppermute | solution.py:12
  44.3 9.4 %collective-permute-start.3 = (f32[64,512]{1,0:T(8,128)S(1)}, f32[64,512]{1,0:T(8,128)S(1)}, u32[]{:S(2)}, u32[]{:S(2)}) collective-permute-start(f32[64,512]{1,0:T(8,128)S(1)} %slice.63), channel_id=1, source_target_pairs={{31,0},{0,1},{1,2},{2,3},{3,4},{4,5},{5,6},{6,7},{7,8},{8,9},{9,10... | collective-permute-start | bytes 393224 | tf_op jit(solution)/shard_map/ppermute | solution.py:12
  56.0 4.7 collective-permute-start.4
  69.8 9.3 %collective-permute-start.5 = (f32[64,512]{1,0:T(8,128)S(1)}, f32[64,512]{1,0:T(8,128)S(1)}, u32[]{:S(2)}, u32[]{:S(2)}) collective-permute-start(f32[64,512]{1,0:T(8,128)S(1)} %slice.65), channel_id=1, source_target_pairs={{31,0},{0,1},{1,2},{2,3},{3,4},{4,5},{5,6},{6,7},{7,8},{8,9},{9,10... | collective-permute-start | bytes 393224 | tf_op jit(solution)/shard_map/ppermute | solution.py:12
  81.3 4.9 collective-permute-start.6
  95.2 9.6 %collective-permute-start.7 = (f32[64,512]{1,0:T(8,128)S(1)}, f32[64,512]{1,0:T(8,128)S(1)}, u32[]{:S(2)}, u32[]{:S(2)}) collective-permute-start(f32[64,512]{1,0:T(8,128)S(1)} %slice.67), channel_id=1, source_target_pairs={{31,0},{0,1},{1,2},{2,3},{3,4},{4,5},{5,6},{6,7},{7,8},{8,9},{9,10... | collective-permute-start | bytes 393224 | tf_op jit(solution)/shard_map/ppermute | solution.py:12
  106.3 186.0 %copy-start.1 = (bf16[256,512]{1,0:T(8,128)(2,1)}, bf16[256,512]{1,0:T(8,128)(2,1)S(1)}, u32[]{:S(2)}) copy-start(bf16[256,512]{1,0:T(8,128)(2,1)S(1)} %get-tuple-element.4) | copy-start | bytes 786436
  106.3 8.5 %collective-permute-start.8 = (bf16[256,512]{1,0:T(8,128)(2,1)S(1)}, bf16[256,512]{1,0:T(8,128)(2,1)S(1)}, u32[]{:S(2)}, u32[]{:S(2)}) collective-permute-start(bf16[256,512]{1,0:T(8,128)(2,1)S(1)} %get-tuple-element.4), channel_id=1, source_target_pairs={{224,0},{0,32},{32,64},{64,96},{96,128},{128,160},{160,192},{192,2... | collective-permute-start | bytes 786440 | tf_op jit(solution)/shard_map/ppermute | solution.py:12
  114.8 8.8 %collective-permute-start.9 = (bf16[256,512]{1,0:T(8,128)(2,1)S(1)}, bf16[256,512]{1,0:T(8,128)(2,1)S(1)}, u32[]{:S(2)}, u32[]{:S(2)}) collective-permute-start(bf16[256,512]{1,0:T(8,128)(2,1)S(1)} %collective-permute-done.8), channel_id=1, source_target_pairs={{224,0},{0,32},{32,64},{64,96},{96,128},{128,160},{160,192},{192,2... | collective-permute-start | bytes 786440 | tf_op jit(solution)/shard_map/ppermute | solution.py:12
  123.6 7.9 %collective-permute-start.10 = (bf16[256,512]{1,0:T(8,128)(2,1)S(1)}, bf16[256,512]{1,0:T(8,128)(2,1)S(1)}, u32[]{:S(2)}, u32[]{:S(2)}) collective-permute-start(bf16[256,512]{1,0:T(8,128)(2,1)S(1)} %collective-permute-done.9), channel_id=1, source_target_pairs={{224,0},{0,32},{32,64},{64,96},{96,128},{128,160},{160,192},{192,2... | collective-permute-start | bytes 786440 | tf_op jit(solution)/shard_map/ppermute | solution.py:12
  131.5 8.0 %collective-permute-start.11 = (bf16[256,512]{1,0:T(8,128)(2,1)S(1)}, bf16[256,512]{1,0:T(8,128)(2,1)S(1)}, u32[]{:S(2)}, u32[]{:S(2)}) collective-permute-start(bf16[256,512]{1,0:T(8,128)(2,1)S(1)} %collective-permute-done.10), channel_id=1, source_target_pairs={{224,0},{0,32},{32,64},{64,96},{96,128},{128,160},{160,192},{192,2... | collective-permute-start | bytes 786440 | tf_op jit(solution)/shard_map/ppermute | solution.py:12
  139.6 10.8 %collective-permute-start.12 = (bf16[256,512]{1,0:T(8,128)(2,1)S(1)}, bf16[256,512]{1,0:T(8,128)(2,1)S(1)}, u32[]{:S(2)}, u32[]{:S(2)}) collective-permute-start(bf16[256,512]{1,0:T(8,128)(2,1)S(1)} %collective-permute-done.11), channel_id=1, source_target_pairs={{224,0},{0,32},{32,64},{64,96},{96,128},{128,160},{160,192},{192,2... | collective-permute-start | bytes 786440 | tf_op jit(solution)/shard_map/ppermute | solution.py:12
  150.4 9.1 %collective-permute-start.13 = (bf16[256,512]{1,0:T(8,128)(2,1)S(1)}, bf16[256,512]{1,0:T(8,128)(2,1)S(1)}, u32[]{:S(2)}, u32[]{:S(2)}) collective-permute-start(bf16[256,512]{1,0:T(8,128)(2,1)S(1)} %collective-permute-done.12), channel_id=1, source_target_pairs={{224,0},{0,32},{32,64},{64,96},{96,128},{128,160},{160,192},{192,2... | collective-permute-start | bytes 786440 | tf_op jit(solution)/shard_map/ppermute | solution.py:12
  159.4 7.9 %collective-permute-start.14 = (bf16[256,512]{1,0:T(8,128)(2,1)S(1)}, bf16[256,512]{1,0:T(8,128)(2,1)S(1)}, u32[]{:S(2)}, u32[]{:S(2)}) collective-permute-start(bf16[256,512]{1,0:T(8,128)(2,1)S(1)} %collective-permute-done.13), channel_id=1, source_target_pairs={{224,0},{0,32},{32,64},{64,96},{96,128},{128,160},{160,192},{192,2... | collective-permute-start | bytes 786440 | tf_op jit(solution)/shard_map/ppermute | solution.py:12
  168.5 367.8 %reduce-scatter.5.cloned.1.call-start = ((), (), s32[]{:S(2)}) async-start(), calls=%async_computation.3 | async-start | bytes 4325376 | tf_op jit(solution)/shard_map/reduce_scatter | solution.py:92
  169.3 4.7 collective-permute-start.15
  181.4 11.4 %collective-permute-start.16 = (f32[64,512]{1,0:T(8,128)S(1)}, f32[64,512]{1,0:T(8,128)S(1)}, u32[]{:S(2)}, u32[]{:S(2)}) collective-permute-start(f32[64,512]{1,0:T(8,128)S(1)} %slice.69), channel_id=1, source_target_pairs={{31,0},{0,1},{1,2},{2,3},{3,4},{4,5},{5,6},{6,7},{7,8},{8,9},{9,10... | collective-permute-start | bytes 393224 | tf_op jit(solution)/shard_map/ppermute | solution.py:12
  194.2 19.0 %collective-permute-start.17 = (bf16[256,512]{1,0:T(8,128)(2,1)S(1)}, bf16[256,512]{1,0:T(8,128)(2,1)S(1)}, u32[]{:S(2)}, u32[]{:S(2)}) collective-permute-start(bf16[256,512]{1,0:T(8,128)(2,1)S(1)} %fusion.2), channel_id=1, source_target_pairs={{224,0},{0,32},{32,64},{64,96},{96,128},{128,160},{160,192},{192,2... | collective-permute-start | bytes 786440 | tf_op jit(solution)/shard_map/ppermute | solution.py:12
  213.1 18.8 %collective-permute-start.18 = (bf16[256,512]{1,0:T(8,128)(2,1)S(1)}, bf16[256,512]{1,0:T(8,128)(2,1)S(1)}, u32[]{:S(2)}, u32[]{:S(2)}) collective-permute-start(bf16[256,512]{1,0:T(8,128)(2,1)S(1)} %collective-permute-done.17), channel_id=1, source_target_pairs={{224,0},{0,32},{32,64},{64,96},{96,128},{128,160},{160,192},{192,2... | collective-permute-start | bytes 786440 | tf_op jit(solution)/shard_map/ppermute | solution.py:12
  231.9 15.0 %collective-permute-start.19 = (bf16[256,512]{1,0:T(8,128)(2,1)S(1)}, bf16[256,512]{1,0:T(8,128)(2,1)S(1)}, u32[]{:S(2)}, u32[]{:S(2)}) collective-permute-start(bf16[256,512]{1,0:T(8,128)(2,1)S(1)} %collective-permute-done.18), channel_id=1, source_target_pairs={{224,0},{0,32},{32,64},{64,96},{96,128},{128,160},{160,192},{192,2... | collective-permute-start | bytes 786440 | tf_op jit(solution)/shard_map/ppermute | solution.py:12
  246.9 10.2 %collective-permute-start.20 = (bf16[256,512]{1,0:T(8,128)(2,1)S(1)}, bf16[256,512]{1,0:T(8,128)(2,1)S(1)}, u32[]{:S(2)}, u32[]{:S(2)}) collective-permute-start(bf16[256,512]{1,0:T(8,128)(2,1)S(1)} %collective-permute-done.19), channel_id=1, source_target_pairs={{224,0},{0,32},{32,64},{64,96},{96,128},{128,160},{160,192},{192,2... | collective-permute-start | bytes 786440 | tf_op jit(solution)/shard_map/ppermute | solution.py:12
  257.1 11.5 %collective-permute-start.21 = (bf16[256,512]{1,0:T(8,128)(2,1)S(1)}, bf16[256,512]{1,0:T(8,128)(2,1)S(1)}, u32[]{:S(2)}, u32[]{:S(2)}) collective-permute-start(bf16[256,512]{1,0:T(8,128)(2,1)S(1)} %collective-permute-done.20), channel_id=1, source_target_pairs={{224,0},{0,32},{32,64},{64,96},{96,128},{128,160},{160,192},{192,2... | collective-permute-start | bytes 786440 | tf_op jit(solution)/shard_map/ppermute | solution.py:12
  268.6 11.7 %collective-permute-start.22 = (bf16[256,512]{1,0:T(8,128)(2,1)S(1)}, bf16[256,512]{1,0:T(8,128)(2,1)S(1)}, u32[]{:S(2)}, u32[]{:S(2)}) collective-permute-start(bf16[256,512]{1,0:T(8,128)(2,1)S(1)} %collective-permute-done.21), channel_id=1, source_target_pairs={{224,0},{0,32},{32,64},{64,96},{96,128},{128,160},{160,192},{192,2... | collective-permute-start | bytes 786440 | tf_op jit(solution)/shard_map/ppermute | solution.py:12
  280.3 12.0 %collective-permute-start.23 = (bf16[256,512]{1,0:T(8,128)(2,1)S(1)}, bf16[256,512]{1,0:T(8,128)(2,1)S(1)}, u32[]{:S(2)}, u32[]{:S(2)}) collective-permute-start(bf16[256,512]{1,0:T(8,128)(2,1)S(1)} %collective-permute-done.22), channel_id=1, source_target_pairs={{224,0},{0,32},{32,64},{64,96},{96,128},{128,160},{160,192},{192,2... | collective-permute-start | bytes 786440 | tf_op jit(solution)/shard_map/ppermute | solution.py:12
Sparse Core Ops, SparseCore 0:
  168.6 187.6 reduce-scatter.2
  358.9 177.4 reduce-scatter.4
where the time goes:
time: 556 us; the launch traced here: 545 us
  waiting for transfers between devices  425 us (76%)
  other arithmetic  33.4 us (6%)
  local copies, waits for them, and re-layouts  29.5 us (5%)
  matrix products  20.6 us (4%)
  starting transfers between devices  20 us (4%)
  between operations  16.5 us (3%)
    ppermute x24, waiting for transfers between devices, shifted(): return lax.ppermute(block, axis, route)  184 us
    reduce_scatter x1, waiting for transfers between devices, shards(): lax.psum_scatter(projected.astype(jnp.bfloat16), 'dom', scatter_dimension...  178 us
    reduce_scatter x1, waiting for transfers between devices, shards(): lax.psum_scatter(intersection.astype(jnp.bfloat16), 'dom', scatter_dimens...  62.8 us
    scatter-add x5, other arithmetic, hamilton(): summed.at[cell_nodes.reshape(-1)].add(cell_out.reshape(-1, columns))  20.3 us
    ppermute x24, starting transfers between devices, shifted(): return lax.ppermute(block, axis, route)  19.9 us
    dot_general x16, matrix products, contract(): lax.dot_general(left, right, (((0,), (0,)), ((), ())), preferred_element_...  19 us
    gather x10, local copies, waits for them, and re-layouts, hamilton(): gathered = extended[cell_nodes]  11.7 us
  transfers between devices with their start and end apart: 26, of which 26 were waited for; matrix products, arithmetic and copies ran while one was open for 7% of the time, Pallas kernels for 0%

commit v1 on v0

v1 whole, which is shorter than its diff:
```python
import jax
import jax.numpy as jnp
from jax import lax
from jax.experimental import pallas as pl
from jax.experimental.pallas import tpu as pltpu
from jax.sharding import PartitionSpec as P

FILTER_DEG = 4
BF = jnp.bfloat16
F32 = jnp.float32
MESH = pl.DeviceIdType.MESH
ORDER = (0, 7, 1, 6, 2, 5, 3, 4)


def nn(a, b):
    return lax.dot_general(a, b, (((1,), (0,)), ((), ())), preferred_element_type=F32)


def nt(a, b):
    return lax.dot_general(a, b, (((1,), (1,)), ((), ())), preferred_element_type=F32)


def split(a):
    hi = a.astype(BF)
    return hi, (a - hi.astype(F32)).astype(BF)


def rows_equal(count, row, base=0):
    index = lax.broadcasted_iota(jnp.int32, (count, row.shape[1]), 0) + base
    return jnp.where(index == row, 1.0, 0.0).astype(BF)


def kernel(
    x_ref, m_ref, ints_ref, vecs_ref, scal_ref,
    filt_ref, inter_ref, proj_ref,
    xp, xc, m2, ints2, vecs2, perm,
    gt0, u0, gt1, u1, kmat, k1, ahi, alo, w2, w2t, kgg_out, kgg_in,
    invb, invl, potb, potl, vcur, vprev, sbuf, gc_out, gc_in,
    fall, fat, p1, r1a, r1b, p2, r2a, r2b, sfin, fin,
    loc_sem, set_s, set_r, kgg_s, kgg_r, halo_s, halo_r,
    zs, zr, cs, cr, rs_s, rs_r,
):
    band = lax.axis_index("band")
    dom = lax.axis_index("dom")
    zh, core = band // 2, band % 2
    zl, x, y = dom % 2, (dom // 2) % 4, dom // 8
    z = zh * 2 + zl

    def device(zz, yy, xx, cc):
        return ((zz // 2) * 2 + cc, (yy * 4 + xx) * 2 + zz % 2)

    z_up, z_down = device((z + 1) % 8, y, x, core), device((z + 7) % 8, y, x, core)
    x_up, x_down = device(z, y, (x + 1) % 4, core), device(z, y, (x + 3) % 4, core)
    y_up, y_down = device(z, (y + 1) % 4, x, core), device(z, (y + 3) % 4, x, core)
    mate = device(z, y, x, 1 - core)
    pair = device(zh * 2 + 1 - zl, y, x, core)
    slab = y * 4 + x
    after, before = (slab + 1) % 16, (slab + 15) % 16
    nxt = device(z, after // 4, after % 4, core)
    prv = device(z, before // 4, before % 4, core)

    barrier = pltpu.get_barrier_semaphore()
    friends = (z_up, z_down, x_up, x_down, y_up, y_down, mate, nxt, prv)
    for friend in friends:
        pl.semaphore_signal(barrier, inc=1, device_id=friend, device_id_type=MESH)

    def send(src, dst, ssem, rsem, to):
        copy = pltpu.make_async_remote_copy(
            src_ref=src, dst_ref=dst, send_sem=ssem, recv_sem=rsem,
            device_id=to, device_id_type=MESH,
        )
        copy.start()
        return copy

    started = []

    col = lax.broadcasted_iota(jnp.int32, (512, 512), 0)
    place = lax.broadcasted_iota(jnp.int32, (512, 512), 1)
    goal = ((col >> 4) & 1) * 256 + (col >> 5) * 16 + (col & 15)
    perm[...] = jnp.where(goal == place, 1.0, 0.0).astype(BF)
    for half in range(2):
        xp[half] = nn(x_ref[...], perm[:, half * 256 : half * 256 + 256]).astype(BF)

    pl.semaphore_wait(barrier, len(friends))
    setup = [
        send(m_ref, m2.at[zl], set_s.at[0], set_r.at[0], pair),
        send(ints_ref, ints2.at[zl], set_s.at[1], set_r.at[1], pair),
        send(vecs_ref, vecs2.at[zl], set_s.at[2], set_r.at[2], pair),
        send(xp.at[1 - zl], xc.at[zl], set_s.at[3], set_r.at[3], pair),
    ]
    started += setup
    own = [
        pltpu.make_async_copy(m_ref, m2.at[zl], loc_sem.at[0]),
        pltpu.make_async_copy(ints_ref, ints2.at[zl], loc_sem.at[1]),
        pltpu.make_async_copy(vecs_ref, vecs2.at[zl], loc_sem.at[2]),
        pltpu.make_async_copy(xp.at[zl], xc.at[zl], loc_sem.at[3]),
    ]
    for copy in own:
        copy.start()
    for copy in own:
        copy.wait()
    kgg_in[64:128] = jnp.zeros((64, 128), F32)
    for copy in setup:
        copy.wait_recv()

    q1t = rows_equal(256, ints2[1, 4:5, :])
    q0t = rows_equal(256, ints2[0, 4:5, :])
    q0t_right = rows_equal(256, ints2[0, 5:6, :])
    for c in range(4):
        lanes = slice(c * 128, c * 128 + 128)
        row = ints2[0, c : c + 1, :]
        top = rows_equal(256, row)
        ghost = rows_equal(128, row, 256)
        bottom = nn(q1t, ghost).astype(BF)
        gt0[0:256, lanes] = top
        gt0[256:512, lanes] = bottom
        u0[0:256, lanes] = nn(top, m2[0, c]).astype(BF)
        u0[256:512, lanes] = nn(bottom, m2[0, c]).astype(BF)
        hot = rows_equal(384, ints2[1, c : c + 1, :])
        gt1[:, lanes] = hot
        u1[:, lanes] = nn(hot, m2[1, c]).astype(BF)
    k1[...] = nt(u1[...], gt1[...])
    kmat[...] = nt(u0[...], gt0[...])
    kmat[256:512, 256:512] += k1[0:256, 0:256]
    kgg_out[...] = k1[256:320, 256:384]
    kgg = send(kgg_out, kgg_in.at[0:64], kgg_s, kgg_r, nxt)
    started.append(kgg)
    w2[0, 0:256] = q0t_right
    w2[1, 0:256] = jnp.zeros((256, 128), BF)
    hi, lo = split(k1[0:256, 256:384])
    w2[0, 256:512] = hi
    w2[1, 256:512] = lo
    eye = jnp.where(
        lax.broadcasted_iota(jnp.int32, (128, 128), 0)
        == lax.broadcasted_iota(jnp.int32, (128, 128), 1),
        1.0,
        0.0,
    ).astype(BF)
    w2t[0, :, 0:256] = nt(eye, q0t_right).astype(BF)
    w2t[1, :, 0:256] = jnp.zeros((128, 256), BF)
    hi, lo = split(k1[256:384, 0:256])
    w2t[0, :, 256:512] = hi
    w2t[1, :, 256:512] = lo

    center, halfwidth = scal_ref[0], scal_ref[1]
    for slot in range(2):
        nodes = slice(slot * 256, slot * 256 + 256)
        columns = jnp.transpose(vecs2[slot])
        mass = jnp.broadcast_to(columns[:, 0:1], (256, 256))
        pot = jnp.broadcast_to(columns[:, 1:2], (256, 256))
        invb[nodes] = mass
        potb[nodes] = pot
        invl[nodes] = mass / halfwidth
        potl[nodes] = (pot - center) / halfwidth
        start = xc[slot].astype(F32)
        vcur[nodes] = start
        sbuf[nodes] = (mass * start).astype(BF)

    def exchange(step):
        out = nn(w2t[0], sbuf[...]) + nn(w2t[1], sbuf[...])
        gc_out[step] = out.astype(BF)
        forth = send(
            gc_out.at[step, 0:64], gc_in.at[step, 64:128],
            halo_s.at[step, 0], halo_r.at[step, 0], nxt,
        )
        back = send(
            gc_out.at[step, 64:128], gc_in.at[step, 0:64],
            halo_s.at[step, 1], halo_r.at[step, 1], prv,
        )
        started.extend([forth, back])
        return forth, back

    def assemble(step, copies):
        inner = nn(ahi[...], sbuf[...]) + nn(alo[...], sbuf[...])
        for copy in copies:
            copy.wait_recv()
        came = gc_in[step]
        return inner + nn(w2[0], came) + nn(w2[1], came)

    copies = exchange(0)
    kgg.wait_recv()
    hi, lo = split(kgg_in[...])
    hi, lo = split(nn(q0t, hi) + nn(q0t, lo))
    kmat[0:256, 0:256] += nt(hi, q0t) + nt(lo, q0t)
    hi, lo = split(kmat[...])
    ahi[...] = hi
    alo[...] = lo

    for step in range(FILTER_DEG):
        if step > 0:
            copies = exchange(step)
        total = assemble(step, copies)
        image = invl[...] * total + potl[...] * vcur[...]
        if step > 0:
            image = 2.0 * image - vprev[...]
        if step < FILTER_DEG - 1:
            vprev[...] = vcur[...]
            vcur[...] = image
            sbuf[...] = (invb[...] * image).astype(BF)
        else:
            filtered = image.astype(BF)
            fall[0, core] = filtered
            wide = filtered.astype(F32)
            vcur[...] = wide
            sbuf[...] = (invb[...] * wide).astype(BF)

    def up(slot, k):
        src, dst = fall.at[slot, core], fall.at[(slot + 7) % 8, core]
        if k == 3:
            src, dst = src.at[0:256], dst.at[0:256]
        started.append(send(src, dst, zs.at[0, k], zr.at[0, k], z_up))
        return started[-1]

    def down(slot, k):
        src, dst = fall.at[slot, core], fall.at[(slot + 1) % 8, core]
        if k == 3:
            src, dst = src.at[256:512], dst.at[256:512]
        started.append(send(src, dst, zs.at[1, k], zr.at[1, k], z_down))
        return started[-1]

    def across(slot):
        block = fall.at[slot, core]
        started.append(send(block, block, cs.at[slot], cr.at[slot], mate))
        return started[-1]

    ups, downs, others = [up(0, 0)], [down(0, 0)], {0: across(0)}

    copies = exchange(FILTER_DEG)
    total = assemble(FILTER_DEG, copies)
    applied = invb[...] * total + potb[...] * vcur[...]
    fat[0:256] = jnp.transpose(vcur[...]).astype(BF)
    vprev[...] = applied
    fat[256:512] = jnp.transpose(vprev[...]).astype(BF)

    def arrive(slot):
        if slot >= 5:
            k = 7 - slot
            ups[k].wait_recv()
            ups.append(up(slot, k + 1))
            others[slot] = across(slot)
        elif 1 <= slot <= 3:
            k = slot - 1
            downs[k].wait_recv()
            downs.append(down(slot, k + 1))
            others[slot] = across(slot)
        elif slot == 4:
            ups[3].wait_recv()
            downs[3].wait_recv()
            others[slot] = across(slot)

    lines = (((x, x_up, x_down), (y, y_up, y_down)), ((y, y_up, y_down), (x, x_up, x_down)))
    flights = {}

    def ring_first(piece, mat, level):
        pos, right, left = lines[mat][level]
        part, in_a = (p1, r1a) if level == 0 else (p2, r2a)
        far = (pos + 2) % 4
        sem = (piece, mat, level)
        pairs = []
        for side, to in ((0, right), (1, left)):
            pairs.append(send(
                part.at[piece, mat, far, side], in_a.at[piece, mat, side],
                rs_s.at[(*sem, side)], rs_r.at[(*sem, side)], to,
            ))
        flights[(*sem, 0)] = pairs
        started.extend(pairs)

    def ring_second(piece, mat, level):
        pos, right, left = lines[mat][level]
        part, in_a, in_b = (p1, r1a, r1b) if level == 0 else (p2, r2a, r2b)
        sem = (piece, mat, level)
        pairs = []
        for side, to in ((0, right), (1, left)):
            near = (pos + 1) % 4 if side == 0 else (pos + 3) % 4
            flights[(*sem, 0)][side].wait_recv()
            whole = part[piece, mat, near, side].astype(F32) + in_a[piece, mat, side].astype(F32)
            part[piece, mat, near, side] = whole.astype(BF)
            pairs.append(send(
                part.at[piece, mat, near], in_b.at[piece, mat, side],
                rs_s.at[(*sem, 2 + side)], rs_r.at[(*sem, 2 + side)], to,
            ))
        flights[(*sem, 1)] = pairs
        started.extend(pairs)

    def ring_last(piece, mat, level):
        pos, right, left = lines[mat][level]
        part, in_b = (p1, r1b) if level == 0 else (p2, r2b)
        for copy in flights[(piece, mat, level, 1)]:
            copy.wait_recv()
        return (
            part[piece, mat, pos].astype(F32)
            + in_b[piece, mat, 0].astype(F32)
            + in_b[piece, mat, 1].astype(F32)
        )

    def stage(number, piece):
        slot = ORDER[piece]
        if number == 0:
            arrive(slot)
            others[slot].wait_recv()
            for side in range(2):
                product = nn(fat[...], fall[slot, side]).astype(BF)
                for yy in range(4):
                    for xx in range(4):
                        k = (yy * 4 + xx) * 16
                        p1[piece, 0, xx, side, yy * 16 : yy * 16 + 16] = product[k : k + 16]
                    k = 256 + yy * 64
                    p1[piece, 1, yy, side] = product[k : k + 64]
            for mat in range(2):
                ring_first(piece, mat, 0)
        elif number == 1:
            for mat in range(2):
                ring_second(piece, mat, 0)
        elif number == 2:
            for mat in range(2):
                level_sum = ring_last(piece, mat, 0).astype(BF)
                for to in range(4):
                    p2[piece, mat, to] = level_sum[:, to * 16 : to * 16 + 16]
                ring_first(piece, mat, 1)
        elif number == 3:
            for mat in range(2):
                ring_second(piece, mat, 1)
        else:
            source = (z + slot) % 8
            for mat in range(2):
                sfin[source, :, mat] = ring_last(piece, mat, 1)

    for tick in range(12):
        for number in range(4, -1, -1):
            piece = tick - number
            if 0 <= piece < 8:
                stage(number, piece)

    mine = pl.ds(pl.multiple_of(zl * 256, 256), 256)
    filt_ref[...] = (
        nt(fall[zl * 7, core, mine], perm[:, 0:256]) + nt(fall[1 - zl, core, mine], perm[:, 256:512])
    ).astype(BF)
    factor = 1.0 / 8192
    for group in range(8):
        lines_of = slice(group * 32, group * 32 + 32)
        for half in range(2):
            block = sfin[(group // 2) * 2 + half, group % 2].reshape(32, 256)
            hi, lo = split(block)
            fin[0, lines_of, half * 256 : half * 256 + 256] = hi
            fin[1, lines_of, half * 256 : half * 256 + 256] = lo
    result = (nt(fin[0], perm[...]) + nt(fin[1], perm[...])) * factor
    for group in range(8):
        lanes = slice(group * 512, group * 512 + 512)
        inter_ref[:, lanes] = result[group * 32 : group * 32 + 16]
        proj_ref[:, lanes] = result[group * 32 + 16 : group * 32 + 32]
    for copy in started:
        copy.wait_send()


def shards(
    orbital_block,
    cell_matrices,
    cell_nodes,
    shared_nodes,
    inv_sqrt_mass,
    potential,
    filter_center,
    filter_halfwidth,
):
    matrices = jnp.pad(cell_matrices, ((0, 0), (0, 3), (0, 3)))
    nodes = jnp.pad(cell_nodes.T, ((0, 0), (0, 3)), constant_values=-1)
    shared = jnp.concatenate(
        [
            jnp.pad(shared_nodes, ((0, 0), (0, 64)), constant_values=-1),
            jnp.pad(shared_nodes, ((0, 0), (64, 0)), constant_values=-1),
        ]
    )
    ints = jnp.pad(jnp.concatenate([nodes, shared]), ((0, 2), (0, 0)), constant_values=-1)
    vecs = jnp.pad(jnp.stack([inv_sqrt_mass, potential]), ((0, 6), (0, 0)))
    scal = jnp.concatenate([filter_center, filter_halfwidth])
    vm = pl.BlockSpec(memory_space=pltpu.VMEM)
    V = pltpu.VMEM
    dma = pltpu.SemaphoreType.DMA
    return pl.pallas_call(
        kernel,
        out_shape=(
            jax.ShapeDtypeStruct((256, 512), BF),
            jax.ShapeDtypeStruct((16, 4096), F32),
            jax.ShapeDtypeStruct((16, 4096), F32),
        ),
        in_specs=[vm, vm, vm, vm, pl.BlockSpec(memory_space=pltpu.SMEM)],
        out_specs=(vm, vm, vm),
        scratch_shapes=[
            V((2, 256, 256), BF),
            V((2, 256, 256), BF),
            V((2, 4, 128, 128), BF),
            V((2, 8, 128), jnp.int32),
            V((2, 8, 256), F32),
            V((512, 512), BF),
            V((512, 512), BF),
            V((512, 512), BF),
            V((384, 512), BF),
            V((384, 512), BF),
            V((512, 512), F32),
            V((384, 384), F32),
            V((512, 512), BF),
            V((512, 512), BF),
            V((2, 512, 128), BF),
            V((2, 128, 512), BF),
            V((64, 128), F32),
            V((128, 128), F32),
            V((512, 256), F32),
            V((512, 256), F32),
            V((512, 256), F32),
            V((512, 256), F32),
            V((512, 256), F32),
            V((512, 256), F32),
            V((512, 256), BF),
            V((FILTER_DEG + 1, 128, 256), BF),
            V((FILTER_DEG + 1, 128, 256), BF),
            V((8, 2, 512, 256), BF),
            V((512, 512), BF),
            V((8, 2, 4, 2, 64, 256), BF),
            V((8, 2, 2, 64, 256), BF),
            V((8, 2, 2, 2, 64, 256), BF),
            V((8, 2, 4, 2, 16, 256), BF),
            V((8, 2, 2, 16, 256), BF),
            V((8, 2, 2, 2, 16, 256), BF),
            V((8, 2, 2, 16, 256), F32),
            V((2, 256, 512), BF),
            dma((4,)),
            dma((4,)),
            dma((4,)),
            dma,
            dma,
            dma((FILTER_DEG + 1, 2)),
            dma((FILTER_DEG + 1, 2)),
            dma((2, 4)),
            dma((2, 4)),
            dma((8,)),
            dma((8,)),
            dma((8, 2, 2, 4)),
            dma((8, 2, 2, 4)),
        ],
        compiler_params=pltpu.CompilerParams(
            collective_id=0, has_side_effects=True, vmem_limit_bytes=56 * 1024 * 1024
        ),
    )(orbital_block, matrices, ints, vecs, scal)


def solution(mesh):
    return jax.shard_map(
        shards,
        mesh=mesh,
        in_specs=(
            P("dom", "band"),
            P("dom", None, None),
            P(None, "dom"),
            P("dom", None),
            P("dom"),
            P("dom"),
            P(),
            P(),
        ),
        out_specs=(P("dom", "band"), P(("band", "dom"), None), P(("band", "dom"), None)),
        check_vma=False,
    )
```

time: 556 us -> 110 us (0.20)
  the two profiles are of different devices: /device:TPU:2 before, /device:TPU:32 now
where the time goes in v1:
time: 110 us
  Pallas kernels  99.8 us (91%)
  local copies, waits for them, and re-layouts  6.45 us (6%)
  between operations  1.95 us (2%)
  other arithmetic  1.33 us (1%)
    pallas_call x1, Pallas kernels, shards(): pl.pallas_call(kernel, out_shape=(jax.ShapeDtypeStruct((256, 512), BF), j...  99.8 us
    unnamed x16, local copies, waits for them, and re-layouts  5.17 us

profile of v1, /device:TPU:32, one launch (start us, length us, event | category | flops | bytes accessed | tf_op | source)
XLA Modules:
  0.0 109.5 jit_solution(16439692592373261784)
XLA Ops:
  1.9 0.7 pad_maximum_fusion.scal_ref
  2.6 0.0 copy-start.2
  2.6 0.0 copy-start.5
  2.6 0.7 copy-done.2
  3.3 0.0 copy-done.5
  3.3 0.1 select_add_fusion
  3.3 0.0 copy-start.3
  3.3 0.0 copy-start.4
  3.3 0.6 pad.28.ints_ref
  3.9 0.1 copy-done.3
  4.0 0.0 copy-done.4
  4.0 0.6 select_maximum_fusion.vecs_ref
  4.6 0.9 copy.11
  5.6 0.7 pad.24.m_ref
  6.3 99.8 %shard_map.103 = (bf16[256,512]{1,0:T(8,128)(2,1)}, f32[16,4096]{1,0:T(8,128)}, f32[16,4096]{1,0:T(8,128)}) custom-call(bf16[256,512]{1,0:T(8,128)(2,1)} %x_ref.1, bf16[4,128,128]{2,1,0:T(8,128)(2,1)} %pad.24.m_ref, s32[8,128]{1,0:T(8,128)} %pad.28.ints_ref, f32[8,256]{1,0:T(8,128)} %select_maximum_fusion.vecs_ref, f32[2]{0:T(128)} %pad_maximum_fusion.scal_ref), custom_call_target="tpu_custom_call" | custom-call | tf_op jit(solution)/shard_map/pallas_call | solution.py:379
  106.1 0.0 copy-start.1
  106.1 1.7 %copy.17 = bf16[256,512]{1,0:T(8,128)(2,1)} copy(bf16[256,512]{1,0:T(8,128)(2,1)} %get-tuple-element.6) | data formatting | bytes 524288
  107.8 0.0 copy-done.1
  107.8 0.0 copy-start
  107.8 0.7 copy.18
  108.5 0.3 copy-done
  108.8 0.7 copy.19
Async XLA Ops:
  2.6 0.7 copy-start.2
  2.6 0.7 copy-start.5
  3.3 0.7 copy-start.3
  3.3 0.7 copy-start.4
  106.1 1.7 %copy-start.1 = (f32[16,4096]{1,0:T(8,128)S(1)}, f32[16,4096]{1,0:T(8,128)}, u32[]{:S(2)}) copy-start(f32[16,4096]{1,0:T(8,128)} %get-tuple-element.7) | copy-start | bytes 786436
  107.8 1.0 copy-start

commit v2 on v1

--- a/solution.py
+++ b/solution.py
@@ -31,9 +31,9 @@
 
 
 def kernel(
-    x_ref, m_ref, ints_ref, vecs_ref, scal_ref,
+    x_ref, m_ref, nodes_ref, shared_ref, mass_ref, pot_ref, center_ref, half_ref,
     filt_ref, inter_ref, proj_ref,
-    xp, xc, m2, ints2, vecs2, perm,
+    mown, ints_own, vecs_own, xp, xc, m2, ints2, vecs2, perm,
     gt0, u0, gt1, u1, kmat, k1, ahi, alo, w2, w2t, kgg_out, kgg_in,
     invb, invl, potb, potl, vcur, vprev, sbuf, gc_out, gc_in,
     fall, fat, p1, r1a, r1b, p2, r2a, r2b, sfin, fin,
@@ -74,33 +74,43 @@
 
     started = []
 
+    ints_own[...] = jnp.full((8, 128), -1, jnp.int32)
+    ints_own[0:4, 0:125] = nodes_ref[...]
+    ints_own[4:5, 0:64] = shared_ref[...]
+    ints_own[5:6, 64:128] = shared_ref[...]
+    vecs_own[...] = jnp.zeros_like(vecs_own)
+    vecs_own[0:1] = mass_ref[...]
+    vecs_own[1:2] = pot_ref[...]
+    mown[...] = jnp.zeros_like(mown)
+    mown[:, 0:125, 0:125] = m_ref[...]
+    kgg_in[64:128] = jnp.zeros((64, 128), F32)
+
+    pl.semaphore_wait(barrier, len(friends))
+    setup = [
+        send(ints_own, ints2.at[zl], set_s.at[0], set_r.at[0], pair),
+        send(vecs_own, vecs2.at[zl], set_s.at[1], set_r.at[1], pair),
+        send(mown, m2.at[zl], set_s.at[2], set_r.at[2], pair),
+    ]
+    own = [
+        pltpu.make_async_copy(ints_own, ints2.at[zl], loc_sem.at[0]),
+        pltpu.make_async_copy(vecs_own, vecs2.at[zl], loc_sem.at[1]),
+        pltpu.make_async_copy(mown, m2.at[zl], loc_sem.at[2]),
+    ]
+    for copy in own:
+        copy.start()
     col = lax.broadcasted_iota(jnp.int32, (512, 512), 0)
     place = lax.broadcasted_iota(jnp.int32, (512, 512), 1)
     goal = ((col >> 4) & 1) * 256 + (col >> 5) * 16 + (col & 15)
     perm[...] = jnp.where(goal == place, 1.0, 0.0).astype(BF)
     for half in range(2):
         xp[half] = nn(x_ref[...], perm[:, half * 256 : half * 256 + 256]).astype(BF)
-
-    pl.semaphore_wait(barrier, len(friends))
-    setup = [
-        send(m_ref, m2.at[zl], set_s.at[0], set_r.at[0], pair),
-        send(ints_ref, ints2.at[zl], set_s.at[1], set_r.at[1], pair),
-        send(vecs_ref, vecs2.at[zl], set_s.at[2], set_r.at[2], pair),
-        send(xp.at[1 - zl], xc.at[zl], set_s.at[3], set_r.at[3], pair),
-    ]
+    setup.append(send(xp.at[1 - zl], xc.at[zl], set_s.at[3], set_r.at[3], pair))
+    own.append(pltpu.make_async_copy(xp.at[zl], xc.at[zl], loc_sem.at[3]))
+    own[3].start()
     started += setup
-    own = [
-        pltpu.make_async_copy(m_ref, m2.at[zl], loc_sem.at[0]),
-        pltpu.make_async_copy(ints_ref, ints2.at[zl], loc_sem.at[1]),
-        pltpu.make_async_copy(vecs_ref, vecs2.at[zl], loc_sem.at[2]),
-        pltpu.make_async_copy(xp.at[zl], xc.at[zl], loc_sem.at[3]),
-    ]
-    for copy in own:
-        copy.start()
-    for copy in own:
+    for copy in own[0:2]:
         copy.wait()
-    kgg_in[64:128] = jnp.zeros((64, 128), F32)
-    for copy in setup:
+    for copy in setup[0:2]:
         copy.wait_recv()
 
     q1t = rows_equal(256, ints2[1, 4:5, :])
@@ -114,17 +124,21 @@
         bottom = nn(q1t, ghost).astype(BF)
         gt0[0:256, lanes] = top
         gt0[256:512, lanes] = bottom
-        u0[0:256, lanes] = nn(top, m2[0, c]).astype(BF)
-        u0[256:512, lanes] = nn(bottom, m2[0, c]).astype(BF)
-        hot = rows_equal(384, ints2[1, c : c + 1, :])
-        gt1[:, lanes] = hot
-        u1[:, lanes] = nn(hot, m2[1, c]).astype(BF)
+        gt1[:, lanes] = rows_equal(384, ints2[1, c : c + 1, :])
+    own[2].wait()
+    setup[2].wait_recv()
+    for c in range(4):
+        lanes = slice(c * 128, c * 128 + 128)
+        u1[:, lanes] = nn(gt1[:, lanes], m2[1, c]).astype(BF)
+    for c in range(4):
+        lanes = slice(c * 128, c * 128 + 128)
+        u0[:, lanes] = nn(gt0[:, lanes], m2[0, c]).astype(BF)
     k1[...] = nt(u1[...], gt1[...])
-    kmat[...] = nt(u0[...], gt0[...])
-    kmat[256:512, 256:512] += k1[0:256, 0:256]
     kgg_out[...] = k1[256:320, 256:384]
     kgg = send(kgg_out, kgg_in.at[0:64], kgg_s, kgg_r, nxt)
     started.append(kgg)
+    kmat[...] = nt(u0[...], gt0[...])
+    kmat[256:512, 256:512] += k1[0:256, 0:256]
     w2[0, 0:256] = q0t_right
     w2[1, 0:256] = jnp.zeros((256, 128), BF)
     hi, lo = split(k1[0:256, 256:384])
@@ -142,7 +156,9 @@
     w2t[0, :, 256:512] = hi
     w2t[1, :, 256:512] = lo
 
-    center, halfwidth = scal_ref[0], scal_ref[1]
+    center, halfwidth = center_ref[0], half_ref[0]
+    own[3].wait()
+    setup[3].wait_recv()
     for slot in range(2):
         nodes = slice(slot * 256, slot * 256 + 256)
         columns = jnp.transpose(vecs2[slot])
@@ -204,49 +220,47 @@
             vcur[...] = wide
             sbuf[...] = (invb[...] * wide).astype(BF)
 
-    def up(slot, k):
-        src, dst = fall.at[slot, core], fall.at[(slot + 7) % 8, core]
-        if k == 3:
-            src, dst = src.at[0:256], dst.at[0:256]
-        started.append(send(src, dst, zs.at[0, k], zr.at[0, k], z_up))
-        return started[-1]
-
-    def down(slot, k):
-        src, dst = fall.at[slot, core], fall.at[(slot + 1) % 8, core]
-        if k == 3:
-            src, dst = src.at[256:512], dst.at[256:512]
-        started.append(send(src, dst, zs.at[1, k], zr.at[1, k], z_down))
-        return started[-1]
-
-    def across(slot):
-        block = fall.at[slot, core]
-        started.append(send(block, block, cs.at[slot], cr.at[slot], mate))
-        return started[-1]
-
-    ups, downs, others = [up(0, 0)], [down(0, 0)], {0: across(0)}
+    tours = ([], [])
+
+    def onward(way, slot, half):
+        landing = (slot + 7) % 8 if way == 0 else (slot + 1) % 8
+        nodes = slice(half * 256, half * 256 + 256)
+        number = len(tours[way])
+        copy = send(
+            fall.at[slot, core, nodes], fall.at[landing, core, nodes],
+            zs.at[way, number], zr.at[way, number], (z_up, z_down)[way],
+        )
+        tours[way].append((copy, landing, half))
+        started.append(copy)
+
+    others = {}
+
+    def across(slot, half):
+        block = fall.at[slot, core, half * 256 : half * 256 + 256]
+        others[slot, half] = send(block, block, cs.at[slot, half], cr.at[slot, half], mate)
+        started.append(others[slot, half])
+
+    def arrive(number):
+        for way in range(2):
+            copy, slot, half = tours[way][number]
+            copy.wait_recv()
+            if number < 5:
+                onward(way, slot, half)
+            across(slot, half)
+
+    for half in range(2):
+        onward(0, 0, half)
+        onward(1, 0, 1 - half)
+    for half in range(2):
+        across(0, half)
 
     copies = exchange(FILTER_DEG)
     total = assemble(FILTER_DEG, copies)
     applied = invb[...] * total + potb[...] * vcur[...]
+    arrive(0)
     fat[0:256] = jnp.transpose(vcur[...]).astype(BF)
     vprev[...] = applied
     fat[256:512] = jnp.transpose(vprev[...]).astype(BF)
-
-    def arrive(slot):
-        if slot >= 5:
-            k = 7 - slot
-            ups[k].wait_recv()
-            ups.append(up(slot, k + 1))
-            others[slot] = across(slot)
-        elif 1 <= slot <= 3:
-            k = slot - 1
-            downs[k].wait_recv()
-            downs.append(down(slot, k + 1))
-            others[slot] = across(slot)
-        elif slot == 4:
-            ups[3].wait_recv()
-            downs[3].wait_recv()
-            others[slot] = across(slot)
 
     lines = (((x, x_up, x_down), (y, y_up, y_down)), ((y, y_up, y_down), (x, x_up, x_down)))
     flights = {}
@@ -296,9 +310,11 @@
     def stage(number, piece):
         slot = ORDER[piece]
         if number == 0:
-            arrive(slot)
-            others[slot].wait_recv()
-            for side in range(2):
+            for turn in range(2):
+                side = core if turn == 0 else 1 - core
+                if turn == 1:
+                    for half in range(2):
+                        others[slot, half].wait_recv()
                 product = nn(fat[...], fall[slot, side]).astype(BF)
                 for yy in range(4):
                     for xx in range(4):
@@ -325,16 +341,20 @@
             for mat in range(2):
                 sfin[source, :, mat] = ring_last(piece, mat, 1)
 
-    for tick in range(12):
+    for tick in range(16):
+        if 1 <= tick <= 6:
+            arrive(tick)
         for number in range(4, -1, -1):
-            piece = tick - number
+            piece = tick - 2 * number
             if 0 <= piece < 8:
                 stage(number, piece)
-
-    mine = pl.ds(pl.multiple_of(zl * 256, 256), 256)
-    filt_ref[...] = (
-        nt(fall[zl * 7, core, mine], perm[:, 0:256]) + nt(fall[1 - zl, core, mine], perm[:, 256:512])
-    ).astype(BF)
+        if tick == 8:
+            mine = pl.ds(pl.multiple_of(zl * 256, 256), 256)
+            filt_ref[...] = (
+                nt(fall[zl * 7, core, mine], perm[:, 0:256])
+                + nt(fall[1 - zl, core, mine], perm[:, 256:512])
+            ).astype(BF)
+
     factor = 1.0 / 8192
     for group in range(8):
         lines_of = slice(group * 32, group * 32 + 32)
@@ -362,18 +382,8 @@
     filter_center,
     filter_halfwidth,
 ):
-    matrices = jnp.pad(cell_matrices, ((0, 0), (0, 3), (0, 3)))
-    nodes = jnp.pad(cell_nodes.T, ((0, 0), (0, 3)), constant_values=-1)
-    shared = jnp.concatenate(
-        [
-            jnp.pad(shared_nodes, ((0, 0), (0, 64)), constant_values=-1),
-            jnp.pad(shared_nodes, ((0, 0), (64, 0)), constant_values=-1),
-        ]
-    )
-    ints = jnp.pad(jnp.concatenate([nodes, shared]), ((0, 2), (0, 0)), constant_values=-1)
-    vecs = jnp.pad(jnp.stack([inv_sqrt_mass, potential]), ((0, 6), (0, 0)))
-    scal = jnp.concatenate([filter_center, filter_halfwidth])
     vm = pl.BlockSpec(memory_space=pltpu.VMEM)
+    sm = pl.BlockSpec(memory_space=pltpu.SMEM)
     V = pltpu.VMEM
     dma = pltpu.SemaphoreType.DMA
     return pl.pallas_call(
@@ -383,9 +393,12 @@
             jax.ShapeDtypeStruct((16, 4096), F32),
             jax.ShapeDtypeStruct((16, 4096), F32),
         ),
-        in_specs=[vm, vm, vm, vm, pl.BlockSpec(memory_space=pltpu.SMEM)],
+        in_specs=[vm, vm, vm, vm, vm, vm, sm, sm],
         out_specs=(vm, vm, vm),
         scratch_shapes=[
+            V((4, 128, 128), BF),
+            V((8, 128), jnp.int32),
+            V((8, 256), F32),
             V((2, 256, 256), BF),
             V((2, 256, 256), BF),
             V((2, 4, 128, 128), BF),
@@ -430,17 +443,26 @@
             dma,
             dma((FILTER_DEG + 1, 2)),
             dma((FILTER_DEG + 1, 2)),
-            dma((2, 4)),
-            dma((2, 4)),
-            dma((8,)),
-            dma((8,)),
+            dma((2, 7)),
+            dma((2, 7)),
+            dma((8, 2)),
+            dma((8, 2)),
             dma((8, 2, 2, 4)),
             dma((8, 2, 2, 4)),
         ],
         compiler_params=pltpu.CompilerParams(
             collective_id=0, has_side_effects=True, vmem_limit_bytes=56 * 1024 * 1024
         ),
-    )(orbital_block, matrices, ints, vecs, scal)
+    )(
+        orbital_block,
+        cell_matrices,
+        cell_nodes.T,
+        shared_nodes,
+        inv_sqrt_mass.reshape(1, 256),
+        potential.reshape(1, 256),
+        filter_center,
+        filter_halfwidth,
+    )
 
 
 def solution(mesh):

time: 110 us -> 90 us (0.82)
  the two profiles are of different devices: /device:TPU:32 before, /device:TPU:2 now
where the time goes in v2:
time: 90 us; the launch traced here: 89.8 us
  Pallas kernels  82.8 us (92%)
  local copies, waits for them, and re-layouts  5.04 us (6%)
  between operations  1.94 us (2%)
    pallas_call x1, Pallas kernels, shards(): pl.pallas_call(kernel, out_shape=(jax.ShapeDtypeStruct((256, 512), BF), j...  82.8 us
    unnamed x8, local copies, waits for them, and re-layouts  5.04 us

profile of v2, /device:TPU:2, one launch (start us, length us, event | category | flops | bytes accessed | tf_op | source)
XLA Modules:
  0.0 89.8 jit_solution(2771636748299245689)
XLA Ops:
  1.9 1.6 %copy.11.m_ref = bf16[4,125,125]{2,1,0:T(8,128)(2,1)} copy(bf16[4,125,125]{2,0,1:T(4,128)(2,1)} %param.9) | data formatting | bytes 250000 | tf_op args[1]
  3.5 82.8 %shard_map.103 = (bf16[256,512]{1,0:T(8,128)(2,1)}, f32[16,4096]{1,0:T(8,128)}, f32[16,4096]{1,0:T(8,128)}) custom-call(bf16[256,512]{1,0:T(8,128)(2,1)} %x_ref.1, bf16[4,125,125]{2,1,0:T(8,128)(2,1)} %copy.11.m_ref, s32[4,125]{1,0:T(4,128)} %bitcast.3, s32[1,64]{1,0:T(1,128)} %shared_ref.1, f32[1,256]{1,0:T(1,128)} %bitcast.4, f32[1,256]{1,0:T(1,128)} %bitcast.5, ...), custom_call_target="tpu_custom_call" | custom-call | tf_op jit(solution)/shard_map/pallas_call | solution.py:389
  86.4 0.0 copy-start.1
  86.4 1.7 %copy.17 = bf16[256,512]{1,0:T(8,128)(2,1)} copy(bf16[256,512]{1,0:T(8,128)(2,1)} %get-tuple-element.6) | data formatting | bytes 524288
  88.1 0.0 copy-done.1
  88.1 0.0 copy-start
  88.1 0.7 copy.18
  88.8 0.3 copy-done
  89.1 0.7 copy.19
Async XLA Ops:
  86.4 1.7 %copy-start.1 = (f32[16,4096]{1,0:T(8,128)S(1)}, f32[16,4096]{1,0:T(8,128)}, u32[]{:S(2)}) copy-start(f32[16,4096]{1,0:T(8,128)} %get-tuple-element.7) | copy-start | bytes 786436
  88.1 1.0 %copy-start = (f32[16,4096]{1,0:T(8,128)S(1)}, f32[16,4096]{1,0:T(8,128)}, u32[]{:S(2)}) copy-start(f32[16,4096]{1,0:T(8,128)} %get-tuple-element.8) | copy-start | bytes 786436

commit v3 on v2

--- a/solution.py
+++ b/solution.py
@@ -34,7 +34,7 @@
     x_ref, m_ref, nodes_ref, shared_ref, mass_ref, pot_ref, center_ref, half_ref,
     filt_ref, inter_ref, proj_ref,
     mown, ints_own, vecs_own, xp, xc, m2, ints2, vecs2, perm,
-    gt0, u0, gt1, u1, kmat, k1, ahi, alo, w2, w2t, kgg_out, kgg_in,
+    gt0, u0, gt1, u1, kmat, k1, ahi, alo, w2, wc, q0, eye, kgg_out, kgg_in,
     invb, invl, potb, potl, vcur, vprev, sbuf, gc_out, gc_in,
     fall, fat, p1, r1a, r1b, p2, r2a, r2b, sfin, fin,
     loc_sem, set_s, set_r, kgg_s, kgg_r, halo_s, halo_r,
@@ -82,14 +82,16 @@
     vecs_own[0:1] = mass_ref[...]
     vecs_own[1:2] = pot_ref[...]
     mown[...] = jnp.zeros_like(mown)
-    mown[:, 0:125, 0:125] = m_ref[...]
+    for c in range(4):
+        mown[c, 0:125, 0:125] = m_ref[:, c, :]
     kgg_in[64:128] = jnp.zeros((64, 128), F32)
 
+    cells = pl.ds(core * 2, 2)
     pl.semaphore_wait(barrier, len(friends))
     setup = [
         send(ints_own, ints2.at[zl], set_s.at[0], set_r.at[0], pair),
         send(vecs_own, vecs2.at[zl], set_s.at[1], set_r.at[1], pair),
-        send(mown, m2.at[zl], set_s.at[2], set_r.at[2], pair),
+        send(mown.at[cells], m2.at[zl, cells], set_s.at[2], set_r.at[2], pair),
     ]
     own = [
         pltpu.make_async_copy(ints_own, ints2.at[zl], loc_sem.at[0]),
@@ -125,8 +127,12 @@
         gt0[0:256, lanes] = top
         gt0[256:512, lanes] = bottom
         gt1[:, lanes] = rows_equal(384, ints2[1, c : c + 1, :])
+    setup[2].wait_recv()
+    half_cells = m2.at[1 - zl, cells]
+    shared_cells = send(half_cells, half_cells, set_s.at[4], set_r.at[4], mate)
+    started.append(shared_cells)
     own[2].wait()
-    setup[2].wait_recv()
+    shared_cells.wait_recv()
     for c in range(4):
         lanes = slice(c * 128, c * 128 + 128)
         u1[:, lanes] = nn(gt1[:, lanes], m2[1, c]).astype(BF)
@@ -140,21 +146,15 @@
     kmat[...] = nt(u0[...], gt0[...])
     kmat[256:512, 256:512] += k1[0:256, 0:256]
     w2[0, 0:256] = q0t_right
-    w2[1, 0:256] = jnp.zeros((256, 128), BF)
     hi, lo = split(k1[0:256, 256:384])
     w2[0, 256:512] = hi
     w2[1, 256:512] = lo
-    eye = jnp.where(
-        lax.broadcasted_iota(jnp.int32, (128, 128), 0)
-        == lax.broadcasted_iota(jnp.int32, (128, 128), 1),
-        1.0,
-        0.0,
-    ).astype(BF)
-    w2t[0, :, 0:256] = nt(eye, q0t_right).astype(BF)
-    w2t[1, :, 0:256] = jnp.zeros((128, 256), BF)
-    hi, lo = split(k1[256:384, 0:256])
-    w2t[0, :, 256:512] = hi
-    w2t[1, :, 256:512] = lo
+    unit = lax.broadcasted_iota(jnp.int32, (256, 256), 0)
+    eye[...] = jnp.where(unit == lax.broadcasted_iota(jnp.int32, (256, 256), 1), 1.0, 0.0).astype(BF)
+    q0[...] = nt(eye[0:128, 0:128], q0t_right)[64:128].astype(BF)
+    hi, lo = split(k1[256:320, 0:256])
+    wc[0] = hi
+    wc[1] = lo
 
     center, halfwidth = center_ref[0], half_ref[0]
     own[3].wait()
@@ -172,28 +172,32 @@
         vcur[nodes] = start
         sbuf[nodes] = (mass * start).astype(BF)
 
-    def exchange(step):
-        out = nn(w2t[0], sbuf[...]) + nn(w2t[1], sbuf[...])
-        gc_out[step] = out.astype(BF)
-        forth = send(
-            gc_out.at[step, 0:64], gc_in.at[step, 64:128],
-            halo_s.at[step, 0], halo_r.at[step, 0], nxt,
+    def push(step, half):
+        if half == 1:
+            out = nn(wc[0], sbuf[256:512]) + nn(wc[1], sbuf[256:512])
+            rows, landing, to = slice(0, 64), slice(64, 128), nxt
+        else:
+            out = nn(q0[...], sbuf[0:256])
+            rows, landing, to = slice(64, 128), slice(0, 64), prv
+        gc_out[step, rows] = out.astype(BF)
+        copy = send(
+            gc_out.at[step, rows], gc_in.at[step, landing],
+            halo_s.at[step, half], halo_r.at[step, half], to,
         )
-        back = send(
-            gc_out.at[step, 64:128], gc_in.at[step, 0:64],
-            halo_s.at[step, 1], halo_r.at[step, 1], prv,
-        )
-        started.extend([forth, back])
-        return forth, back
-
-    def assemble(step, copies):
-        inner = nn(ahi[...], sbuf[...]) + nn(alo[...], sbuf[...])
-        for copy in copies:
-            copy.wait_recv()
-        came = gc_in[step]
-        return inner + nn(w2[0], came) + nn(w2[1], came)
-
-    copies = exchange(0)
+        started.append(copy)
+        return copy
+
+    def inside():
+        return nn(ahi[...], sbuf[...]) + nn(alo[...], sbuf[...])
+
+    def whole(inner, half, came):
+        nodes = slice(half * 256, half * 256 + 256)
+        total = inner[nodes] + nn(w2[0, nodes], came)
+        if half == 1:
+            total = total + nn(w2[1, nodes], came)
+        return nodes, total
+
+    copies = [push(0, 1), push(0, 0)]
     kgg.wait_recv()
     hi, lo = split(kgg_in[...])
     hi, lo = split(nn(q0t, hi) + nn(q0t, lo))
@@ -203,28 +207,31 @@
     alo[...] = lo
 
     for step in range(FILTER_DEG):
-        if step > 0:
-            copies = exchange(step)
-        total = assemble(step, copies)
-        image = invl[...] * total + potl[...] * vcur[...]
-        if step > 0:
-            image = 2.0 * image - vprev[...]
-        if step < FILTER_DEG - 1:
-            vprev[...] = vcur[...]
-            vcur[...] = image
-            sbuf[...] = (invb[...] * image).astype(BF)
-        else:
-            filtered = image.astype(BF)
-            fall[0, core] = filtered
-            wide = filtered.astype(F32)
-            vcur[...] = wide
-            sbuf[...] = (invb[...] * wide).astype(BF)
+        inner = inside()
+        for copy in copies:
+            copy.wait_recv()
+        came = gc_in[step]
+        copies = []
+        for half in (1, 0):
+            nodes, total = whole(inner, half, came)
+            image = invl[nodes] * total + potl[nodes] * vcur[nodes]
+            if step > 0:
+                image = 2.0 * image - vprev[nodes]
+            if step < FILTER_DEG - 1:
+                vprev[nodes] = vcur[nodes]
+            else:
+                filtered = image.astype(BF)
+                fall[0, core, nodes] = filtered
+                image = filtered.astype(F32)
+            vcur[nodes] = image
+            sbuf[nodes] = (invb[nodes] * image).astype(BF)
+            copies.append(push(step + 1, half))
 
     tours = ([], [])
 
     def onward(way, slot, half):
         landing = (slot + 7) % 8 if way == 0 else (slot + 1) % 8
-        nodes = slice(half * 256, half * 256 + 256)
+        nodes = slice(half * 128, half * 128 + 128)
         number = len(tours[way])
         copy = send(
             fall.at[slot, core, nodes], fall.at[landing, core, nodes],
@@ -236,7 +243,7 @@
     others = {}
 
     def across(slot, half):
-        block = fall.at[slot, core, half * 256 : half * 256 + 256]
+        block = fall.at[slot, core, half * 128 : half * 128 + 128]
         others[slot, half] = send(block, block, cs.at[slot, half], cr.at[slot, half], mate)
         started.append(others[slot, half])
 
@@ -244,29 +251,20 @@
         for way in range(2):
             copy, slot, half = tours[way][number]
             copy.wait_recv()
-            if number < 5:
+            if number < 10:
                 onward(way, slot, half)
             across(slot, half)
 
-    for half in range(2):
+    for half in range(4):
         onward(0, 0, half)
-        onward(1, 0, 1 - half)
-    for half in range(2):
+        onward(1, 0, 3 - half)
         across(0, half)
-
-    copies = exchange(FILTER_DEG)
-    total = assemble(FILTER_DEG, copies)
-    applied = invb[...] * total + potb[...] * vcur[...]
-    arrive(0)
-    fat[0:256] = jnp.transpose(vcur[...]).astype(BF)
-    vprev[...] = applied
-    fat[256:512] = jnp.transpose(vprev[...]).astype(BF)
 
     lines = (((x, x_up, x_down), (y, y_up, y_down)), ((y, y_up, y_down), (x, x_up, x_down)))
     flights = {}
 
     def ring_first(piece, mat, level):
-        pos, right, left = lines[mat][level]
+        pos, right, left = lines[mat ^ (piece & 1)][level]
         part, in_a = (p1, r1a) if level == 0 else (p2, r2a)
         far = (pos + 2) % 4
         sem = (piece, mat, level)
@@ -280,7 +278,7 @@
         started.extend(pairs)
 
     def ring_second(piece, mat, level):
-        pos, right, left = lines[mat][level]
+        pos, right, left = lines[mat ^ (piece & 1)][level]
         part, in_a, in_b = (p1, r1a, r1b) if level == 0 else (p2, r2a, r2b)
         sem = (piece, mat, level)
         pairs = []
@@ -297,7 +295,7 @@
         started.extend(pairs)
 
     def ring_last(piece, mat, level):
-        pos, right, left = lines[mat][level]
+        pos, right, left = lines[mat ^ (piece & 1)][level]
         part, in_b = (p1, r1b) if level == 0 else (p2, r2b)
         for copy in flights[(piece, mat, level, 1)]:
             copy.wait_recv()
@@ -307,21 +305,30 @@
             + in_b[piece, mat, 1].astype(F32)
         )
 
+    def place(product, piece, mat, side):
+        for yy in range(4):
+            k = yy * 64
+            if mat ^ (piece & 1):
+                p1[piece, mat, yy, side] = product[k : k + 64]
+            else:
+                for xx in range(4):
+                    rows = product[k + xx * 16 : k + xx * 16 + 16]
+                    p1[piece, mat, xx, side, yy * 16 : yy * 16 + 16] = rows
+
+    def landed(slot):
+        for part in range(4):
+            others[slot, part].wait_recv()
+
     def stage(number, piece):
         slot = ORDER[piece]
         if number == 0:
             for turn in range(2):
                 side = core if turn == 0 else 1 - core
                 if turn == 1:
-                    for half in range(2):
-                        others[slot, half].wait_recv()
+                    landed(slot)
                 product = nn(fat[...], fall[slot, side]).astype(BF)
-                for yy in range(4):
-                    for xx in range(4):
-                        k = (yy * 4 + xx) * 16
-                        p1[piece, 0, xx, side, yy * 16 : yy * 16 + 16] = product[k : k + 16]
-                    k = 256 + yy * 64
-                    p1[piece, 1, yy, side] = product[k : k + 64]
+                for mat in range(2):
+                    place(product[mat * 256 : mat * 256 + 256], piece, mat, side)
             for mat in range(2):
                 ring_first(piece, mat, 0)
         elif number == 1:
@@ -341,21 +348,43 @@
             for mat in range(2):
                 sfin[source, :, mat] = ring_last(piece, mat, 1)
 
-    for tick in range(16):
-        if 1 <= tick <= 6:
-            arrive(tick)
+    inner = inside()
+    fat[0:256] = nt(eye[...], fall[0, core]).astype(BF)
+    place(nn(fat[0:256], fall[0, core]).astype(BF), 0, 0, core)
+    landed(0)
+    place(nn(fat[0:256], fall[0, 1 - core]).astype(BF), 0, 0, 1 - core)
+    ring_first(0, 0, 0)
+    arrive(0)
+    for copy in copies:
+        copy.wait_recv()
+    came = gc_in[FILTER_DEG]
+    for half in (1, 0):
+        nodes, total = whole(inner, half, came)
+        sbuf[nodes] = (invb[nodes] * total + potb[nodes] * vcur[nodes]).astype(BF)
+    arrive(1)
+    fat[256:512] = nt(eye[...], sbuf[...]).astype(BF)
+    for side in range(2):
+        place(nn(fat[256:512], fall[0, side]).astype(BF), 0, 1, side)
+    ring_first(0, 1, 0)
+    arrive(2)
+
+    ahead = {1: (3,), 3: (7,), 5: (11,)}
+    behind = {1: (4,), 2: (5, 6), 3: (8,), 4: (9, 10), 5: (12,), 6: (13,)}
+    for tick in range(1, 16):
+        for number in ahead.get(tick, ()):
+            arrive(number)
         for number in range(4, -1, -1):
             piece = tick - 2 * number
             if 0 <= piece < 8:
                 stage(number, piece)
+        for number in behind.get(tick, ()):
+            arrive(number)
         if tick == 8:
             mine = pl.ds(pl.multiple_of(zl * 256, 256), 256)
-            filt_ref[...] = (
-                nt(fall[zl * 7, core, mine], perm[:, 0:256])
-                + nt(fall[1 - zl, core, mine], perm[:, 256:512])
-            ).astype(BF)
-
-    factor = 1.0 / 8192
+            filt_ref[...] = nt(fall[zl * 7, core, mine], perm[:, 0:256]) + nt(
+                fall[1 - zl, core, mine], perm[:, 256:512]
+            )
+
     for group in range(8):
         lines_of = slice(group * 32, group * 32 + 32)
         for half in range(2):
@@ -363,7 +392,7 @@
             hi, lo = split(block)
             fin[0, lines_of, half * 256 : half * 256 + 256] = hi
             fin[1, lines_of, half * 256 : half * 256 + 256] = lo
-    result = (nt(fin[0], perm[...]) + nt(fin[1], perm[...])) * factor
+    result = nt(fin[0], perm[...]) + nt(fin[1], perm[...])
     for group in range(8):
         lanes = slice(group * 512, group * 512 + 512)
         inter_ref[:, lanes] = result[group * 32 : group * 32 + 16]
@@ -386,10 +415,10 @@
     sm = pl.BlockSpec(memory_space=pltpu.SMEM)
     V = pltpu.VMEM
     dma = pltpu.SemaphoreType.DMA
-    return pl.pallas_call(
+    filtered, intersection, projected = pl.pallas_call(
         kernel,
         out_shape=(
-            jax.ShapeDtypeStruct((256, 512), BF),
+            jax.ShapeDtypeStruct((256, 512), F32),
             jax.ShapeDtypeStruct((16, 4096), F32),
             jax.ShapeDtypeStruct((16, 4096), F32),
         ),
@@ -414,7 +443,9 @@
             V((512, 512), BF),
             V((512, 512), BF),
             V((2, 512, 128), BF),
-            V((2, 128, 512), BF),
+            V((2, 64, 256), BF),
+            V((64, 256), BF),
+            V((256, 256), BF),
             V((64, 128), F32),
             V((128, 128), F32),
             V((512, 256), F32),
@@ -437,16 +468,16 @@
             V((8, 2, 2, 16, 256), F32),
             V((2, 256, 512), BF),
             dma((4,)),
-            dma((4,)),
-            dma((4,)),
+            dma((5,)),
+            dma((5,)),
             dma,
             dma,
             dma((FILTER_DEG + 1, 2)),
             dma((FILTER_DEG + 1, 2)),
-            dma((2, 7)),
-            dma((2, 7)),
-            dma((8, 2)),
-            dma((8, 2)),
+            dma((2, 14)),
+            dma((2, 14)),
+            dma((8, 4)),
+            dma((8, 4)),
             dma((8, 2, 2, 4)),
             dma((8, 2, 2, 4)),
         ],
@@ -455,7 +486,7 @@
         ),
     )(
         orbital_block,
-        cell_matrices,
+        jnp.transpose(cell_matrices, (1, 0, 2)),
         cell_nodes.T,
         shared_nodes,
         inv_sqrt_mass.reshape(1, 256),
@@ -463,6 +494,8 @@
         filter_center,
         filter_halfwidth,
     )
+    factor = 1.0 / 8192
+    return filtered.astype(BF), intersection * factor, projected * factor
 
 
 def solution(mesh):

time: 90 us -> 86.2 us (0.958)
  local copies, waits for them, and re-layouts: 5.04 us -> 0.01 us
  other arithmetic: 0 us -> 2.66 us
  Pallas kernels: 82.8 us -> 81.3 us
    unnamed x8 -> x4, local copies, waits for them, and re-layouts: 5.04 us -> 0.01 us
    convert_element_type x0 -> x1, other arithmetic: none -> 1.83 us  [shards(): return (filtered.astype(BF), intersection * factor, projected * factor)]
    pallas_call x1, Pallas kernels: 82.8 us -> 81.3 us  [shards(): pl.pallas_call(kernel, out_shape=(jax.ShapeDtypeStruct((256, 512), F32),...]
where the time goes in v3:
time: 86.2 us; the launch traced here: 86 us
  Pallas kernels  81.3 us (94%)
  other arithmetic  2.66 us (3%)
  between operations  1.95 us (2%)
    pallas_call x1, Pallas kernels, shards(): pl.pallas_call(kernel, out_shape=(jax.ShapeDtypeStruct((256, 512), F32),...  81.3 us
    convert_element_type x1, other arithmetic, shards(): return (filtered.astype(BF), intersection * factor, projected * factor)  1.83 us

profile of v3, /device:TPU:2, one launch (start us, length us, event | category | flops | bytes accessed | tf_op | source)
XLA Modules:
  0.0 86.0 jit_solution(3131055711012828609)
XLA Ops:
  1.9 81.3 %shard_map.103 = (f32[256,512]{1,0:T(8,128)}, f32[16,4096]{1,0:T(8,128)}, f32[16,4096]{1,0:T(8,128)}) custom-call(bf16[256,512]{1,0:T(8,128)(2,1)} %x_ref.1, bf16[125,4,125]{2,1,0:T(4,128)(2,1)} %bitcast.4, s32[4,125]{1,0:T(4,128)} %bitcast.5, s32[1,64]{1,0:T(1,128)} %shared_ref.1, f32[1,256]{1,0:T(1,128)} %bitcast.6, f32[1,256]{1,0:T(1,128)} %bitcast.7, ...), custom_call_target="tpu_custom_call" | custom-call | tf_op jit(solution)/shard_map/pallas_call | solution.py:418
  83.3 0.0 copy-start
  83.3 0.0 copy-start.1
  83.3 1.8 %convert_element_type.3 = bf16[256,512]{1,0:T(8,128)(2,1)} convert(f32[256,512]{1,0:T(8,128)} %get-tuple-element.6) | non-fusion elementwise | flops 131072 | bytes 786432 | tf_op jit(solution)/shard_map/convert_element_type | solution.py:498
  85.1 0.0 copy-done
  85.1 0.0 copy-done.1
  85.1 0.8 broadcast_multiply_fusion
Async XLA Ops:
  83.3 1.9 %copy-start = (f32[16,4096]{1,0:T(8,128)S(1)}, f32[16,4096]{1,0:T(8,128)}, u32[]{:S(2)}) copy-start(f32[16,4096]{1,0:T(8,128)} %get-tuple-element.7) | copy-start | bytes 786436
  83.3 1.8 %copy-start.1 = (f32[16,4096]{1,0:T(8,128)S(1)}, f32[16,4096]{1,0:T(8,128)}, u32[]{:S(2)}) copy-start(f32[16,4096]{1,0:T(8,128)} %get-tuple-element.8) | copy-start | bytes 786436

commit v4 on v3

--- a/solution.py
+++ b/solution.py
@@ -31,9 +31,9 @@
 
 
 def kernel(
-    x_ref, m_ref, nodes_ref, shared_ref, mass_ref, pot_ref, center_ref, half_ref,
+    x_hbm, m_hbm, nodes_hbm, shared_hbm, mass_hbm, pot_hbm, center_ref, half_ref,
     filt_ref, inter_ref, proj_ref,
-    mown, ints_own, vecs_own, xp, xc, m2, ints2, vecs2, perm,
+    x_ref, m_ref, nodes_ref, shared_ref, mass_ref, pot_ref, mown, ints_own, vecs_own, xp, xc, m2, ints2, vecs2, perm,
     gt0, u0, gt1, u1, kmat, k1, ahi, alo, w2, wc, q0, eye, kgg_out, kgg_in,
     invb, invl, potb, potl, vcur, vprev, sbuf, gc_out, gc_in,
     fall, fat, p1, r1a, r1b, p2, r2a, r2b, sfin, fin,
@@ -74,18 +74,29 @@
 
     started = []
 
+    brought = [
+        pltpu.make_async_copy(src, dst, loc_sem.at[4 + number])
+        for number, (src, dst) in enumerate((
+            (nodes_hbm, nodes_ref), (shared_hbm, shared_ref), (mass_hbm, mass_ref),
+            (pot_hbm, pot_ref), (m_hbm, m_ref), (x_hbm, x_ref),
+        ))
+    ]
+    for copy in brought:
+        copy.start()
     ints_own[...] = jnp.full((8, 128), -1, jnp.int32)
+    vecs_own[...] = jnp.zeros_like(vecs_own)
+    mown[...] = jnp.zeros_like(mown)
+    kgg_in[64:128] = jnp.zeros((64, 128), F32)
+    for copy in brought[0:4]:
+        copy.wait()
     ints_own[0:4, 0:125] = nodes_ref[...]
     ints_own[4:5, 0:64] = shared_ref[...]
     ints_own[5:6, 64:128] = shared_ref[...]
-    vecs_own[...] = jnp.zeros_like(vecs_own)
     vecs_own[0:1] = mass_ref[...]
     vecs_own[1:2] = pot_ref[...]
-    mown[...] = jnp.zeros_like(mown)
+    brought[4].wait()
     for c in range(4):
         mown[c, 0:125, 0:125] = m_ref[:, c, :]
-    kgg_in[64:128] = jnp.zeros((64, 128), F32)
-
     cells = pl.ds(core * 2, 2)
     pl.semaphore_wait(barrier, len(friends))
     setup = [
@@ -100,6 +111,7 @@
     ]
     for copy in own:
         copy.start()
+    brought[5].wait()
     col = lax.broadcasted_iota(jnp.int32, (512, 512), 0)
     place = lax.broadcasted_iota(jnp.int32, (512, 512), 1)
     goal = ((col >> 4) & 1) * 256 + (col >> 5) * 16 + (col & 15)
@@ -240,12 +252,14 @@
         tours[way].append((copy, landing, half))
         started.append(copy)
 
-    others = {}
+    others, pieces_in = {}, {}
 
     def across(slot, half):
-        block = fall.at[slot, core, half * 128 : half * 128 + 128]
-        others[slot, half] = send(block, block, cs.at[slot, half], cr.at[slot, half], mate)
-        started.append(others[slot, half])
+        pieces_in[slot] = pieces_in.get(slot, 0) + 1
+        if pieces_in[slot] == 4:
+            block = fall.at[slot, core]
+            others[slot] = send(block, block, cs.at[slot, 0], cr.at[slot, 0], mate)
+            started.append(others[slot])
 
     def arrive(number):
         for way in range(2):
@@ -316,8 +330,7 @@
                     p1[piece, mat, xx, side, yy * 16 : yy * 16 + 16] = rows
 
     def landed(slot):
-        for part in range(4):
-            others[slot, part].wait_recv()
+        others[slot].wait_recv()
 
     def stage(number, piece):
         slot = ORDER[piece]
@@ -413,6 +426,7 @@
 ):
     vm = pl.BlockSpec(memory_space=pltpu.VMEM)
     sm = pl.BlockSpec(memory_space=pltpu.SMEM)
+    hbm = pl.BlockSpec(memory_space=pltpu.HBM)
     V = pltpu.VMEM
     dma = pltpu.SemaphoreType.DMA
     filtered, intersection, projected = pl.pallas_call(
@@ -422,9 +436,15 @@
             jax.ShapeDtypeStruct((16, 4096), F32),
             jax.ShapeDtypeStruct((16, 4096), F32),
         ),
-        in_specs=[vm, vm, vm, vm, vm, vm, sm, sm],
+        in_specs=[hbm] * 6 + [sm, sm],
         out_specs=(vm, vm, vm),
         scratch_shapes=[
+            V((256, 512), BF),
+            V((125, 4, 125), BF),
+            V((4, 125), jnp.int32),
+            V((1, 64), jnp.int32),
+            V((1, 256), F32),
+            V((1, 256), F32),
             V((4, 128, 128), BF),
             V((8, 128), jnp.int32),
             V((8, 256), F32),
@@ -467,7 +487,7 @@
             V((8, 2, 2, 2, 16, 256), BF),
             V((8, 2, 2, 16, 256), F32),
             V((2, 256, 512), BF),
-            dma((4,)),
+            dma((10,)),
             dma((5,)),
             dma((5,)),
             dma,
@@ -482,15 +502,20 @@
             dma((8, 2, 2, 4)),
         ],
         compiler_params=pltpu.CompilerParams(
-            collective_id=0, has_side_effects=True, vmem_limit_bytes=56 * 1024 * 1024
+            collective_id=0, has_side_effects=True, vmem_limit_bytes=28 * 1024 * 1024
         ),
     )(
-        orbital_block,
-        jnp.transpose(cell_matrices, (1, 0, 2)),
-        cell_nodes.T,
-        shared_nodes,
-        inv_sqrt_mass.reshape(1, 256),
-        potential.reshape(1, 256),
+        *(
+            pltpu.with_memory_space_constraint(array, pltpu.HBM)
+            for array in (
+                orbital_block,
+                jnp.transpose(cell_matrices, (1, 0, 2)),
+                cell_nodes.T,
+                shared_nodes,
+                inv_sqrt_mass.reshape(1, 256),
+                potential.reshape(1, 256),
+            )
+        ),
         filter_center,
         filter_halfwidth,
     )

time: 86.2 us -> 83.1 us (0.964)
  Pallas kernels: 81.3 us -> 79.5 us
  other arithmetic: 2.66 us -> 1.56 us
    pallas_call x1, Pallas kernels: 81.3 us -> 79.5 us  [shards(): pl.pallas_call(kernel, out_shape=(jax.ShapeDtypeStruct((256, 512), F32),...]
    convert_element_type x1, other arithmetic: 1.83 us -> 0.74 us  [shards(): return (filtered.astype(BF), intersection * factor, projected * factor)]
where the time goes in v4:
time: 83.1 us; the launch traced here: 83 us
  Pallas kernels  79.5 us (96%)
  between operations  1.93 us (2%)
  other arithmetic  1.56 us (2%)
    pallas_call x1, Pallas kernels, shards(): pl.pallas_call(kernel, out_shape=(jax.ShapeDtypeStruct((256, 512), F32),...  79.5 us

profile of v4, /device:TPU:2, one launch (start us, length us, event | category | flops | bytes accessed | tf_op | source)
XLA Modules:
  0.0 83.0 jit_solution(11498995237821534082)
XLA Ops:
  1.9 79.5 %shard_map.103 = (f32[256,512]{1,0:T(8,128)S(1)}, f32[16,4096]{1,0:T(8,128)S(1)}, f32[16,4096]{1,0:T(8,128)S(1)}) custom-call(bf16[256,512]{1,0:T(8,128)(2,1)} %x_hbm.1, bf16[125,4,125]{2,1,0:T(4,128)(2,1)} %bitcast.4, s32[4,125]{1,0:T(4,128)} %bitcast.5, s32[1,64]{1,0:T(1,128)} %shared_hbm.1, f32[1,256]{1,0:T(1,128)} %bitcast.6, f32[1,256]{1,0:T(1,128)} %bitcast.7, ...), custom_call_target="tpu_custom_call" | custom-call | tf_op jit(solution)/shard_map/pallas_call | solution.py:432
  81.4 0.7 convert_element_type.3
  82.2 0.8 broadcast_multiply_fusion

commit v5 on v4

--- a/solution.py
+++ b/solution.py
@@ -34,7 +34,7 @@
     x_hbm, m_hbm, nodes_hbm, shared_hbm, mass_hbm, pot_hbm, center_ref, half_ref,
     filt_ref, inter_ref, proj_ref,
     x_ref, m_ref, nodes_ref, shared_ref, mass_ref, pot_ref, mown, ints_own, vecs_own, xp, xc, m2, ints2, vecs2, perm,
-    gt0, u0, gt1, u1, kmat, k1, ahi, alo, w2, wc, q0, eye, kgg_out, kgg_in,
+    gt0, u0, gt1, u1, kmat, k1, ahi, alo, w2, wc, q0, eye, kgg_out, kgg_in, first_out,
     invb, invl, potb, potl, vcur, vprev, sbuf, gc_out, gc_in,
     fall, fat, p1, r1a, r1b, p2, r2a, r2b, sfin, fin,
     loc_sem, set_s, set_r, kgg_s, kgg_r, halo_s, halo_r,
@@ -60,7 +60,11 @@
     prv = device(z, before // 4, before % 4, core)
 
     barrier = pltpu.get_barrier_semaphore()
-    friends = (z_up, z_down, x_up, x_down, y_up, y_down, mate, nxt, prv)
+    nxt_across = device(zh * 2 + 1 - zl, after // 4, after % 4, core)
+    prv_across = device(zh * 2 + 1 - zl, before // 4, before % 4, core)
+    friends = (
+        z_up, z_down, x_up, x_down, y_up, y_down, mate, nxt, prv, nxt_across, prv_across,
+    )
     for friend in friends:
         pl.semaphore_signal(barrier, inc=1, device_id=friend, device_id_type=MESH)
 
@@ -86,7 +90,7 @@
     ints_own[...] = jnp.full((8, 128), -1, jnp.int32)
     vecs_own[...] = jnp.zeros_like(vecs_own)
     mown[...] = jnp.zeros_like(mown)
-    kgg_in[64:128] = jnp.zeros((64, 128), F32)
+    kgg_in[1, 64:128] = jnp.zeros((64, 128), F32)
     for copy in brought[0:4]:
         copy.wait()
     ints_own[0:4, 0:125] = nodes_ref[...]
@@ -122,6 +126,36 @@
     own.append(pltpu.make_async_copy(xp.at[zl], xc.at[zl], loc_sem.at[3]))
     own[3].start()
     started += setup
+    for c in range(4):
+        lanes = slice(c * 128, c * 128 + 128)
+        hot = rows_equal(384, ints_own[c : c + 1, :])
+        gt1[:, lanes] = hot
+        u1[256:384, lanes] = nn(hot[256:384], mown[c]).astype(BF)
+    edge = nt(u1[256:384, :], gt1[...])
+    kgg_out[...] = edge[0:64, 256:384]
+    edge_hi, edge_lo = split(edge[0:64, 0:256])
+    unit = lax.broadcasted_iota(jnp.int32, (256, 256), 0)
+    eye[...] = jnp.where(unit == lax.broadcasted_iota(jnp.int32, (256, 256), 1), 1.0, 0.0).astype(BF)
+    pick = nt(eye[0:128, 0:128], rows_equal(256, ints_own[4:5, :]))[0:64].astype(BF)
+    mass_own = jnp.broadcast_to(jnp.transpose(vecs_own[...])[:, 0:1], (256, 256))
+    for half in range(2):
+        scaled = (mass_own * xp[half].astype(F32)).astype(BF)
+        first_out[0, half] = nn(pick, scaled).astype(BF)
+        first_out[1, half] = (nn(edge_hi, scaled) + nn(edge_lo, scaled)).astype(BF)
+    outer = zl * after + (1 - zl) * before
+    landing = pl.ds(pl.multiple_of(zl * 64, 64), 64)
+    kggs = []
+    copies = []
+    for half in range(2):
+        to = device(zh * 2 + half, outer // 4, outer % 4, core)
+        kggs.append(send(
+            kgg_out, kgg_in.at[zl, 0:64], kgg_s.at[half], kgg_r.at[zl], to
+        ))
+        copies.append(send(
+            first_out.at[zl, half], gc_in.at[0, landing],
+            halo_s.at[0, half], halo_r.at[0, zl], to,
+        ))
+    started += kggs + copies
     for copy in own[0:2]:
         copy.wait()
     for copy in setup[0:2]:
@@ -152,17 +186,12 @@
         lanes = slice(c * 128, c * 128 + 128)
         u0[:, lanes] = nn(gt0[:, lanes], m2[0, c]).astype(BF)
     k1[...] = nt(u1[...], gt1[...])
-    kgg_out[...] = k1[256:320, 256:384]
-    kgg = send(kgg_out, kgg_in.at[0:64], kgg_s, kgg_r, nxt)
-    started.append(kgg)
     kmat[...] = nt(u0[...], gt0[...])
     kmat[256:512, 256:512] += k1[0:256, 0:256]
     w2[0, 0:256] = q0t_right
     hi, lo = split(k1[0:256, 256:384])
     w2[0, 256:512] = hi
     w2[1, 256:512] = lo
-    unit = lax.broadcasted_iota(jnp.int32, (256, 256), 0)
-    eye[...] = jnp.where(unit == lax.broadcasted_iota(jnp.int32, (256, 256), 1), 1.0, 0.0).astype(BF)
     q0[...] = nt(eye[0:128, 0:128], q0t_right)[64:128].astype(BF)
     hi, lo = split(k1[256:320, 0:256])
     wc[0] = hi
@@ -209,9 +238,19 @@
             total = total + nn(w2[1, nodes], came)
         return nodes, total
 
-    copies = [push(0, 1), push(0, 0)]
-    kgg.wait_recv()
-    hi, lo = split(kgg_in[...])
+    def expected(src, dst, rsem):
+        return pltpu.make_async_remote_copy(
+            src_ref=src, dst_ref=dst, send_sem=halo_s.at[0, 0], recv_sem=rsem,
+            device_id=nxt, device_id_type=MESH,
+        )
+
+    for side in range(2):
+        expected(kgg_out, kgg_in.at[side, 0:64], kgg_r.at[side]).wait_recv()
+    copies = [
+        expected(first_out.at[0, 0], gc_in.at[0, side * 64 : side * 64 + 64], halo_r.at[0, side])
+        for side in range(2)
+    ]
+    hi, lo = split(kgg_in[1])
     hi, lo = split(nn(q0t, hi) + nn(q0t, lo))
     kmat[0:256, 0:256] += nt(hi, q0t) + nt(lo, q0t)
     hi, lo = split(kmat[...])
@@ -252,14 +291,12 @@
         tours[way].append((copy, landing, half))
         started.append(copy)
 
-    others, pieces_in = {}, {}
+    others = {}
 
     def across(slot, half):
-        pieces_in[slot] = pieces_in.get(slot, 0) + 1
-        if pieces_in[slot] == 4:
-            block = fall.at[slot, core]
-            others[slot] = send(block, block, cs.at[slot, 0], cr.at[slot, 0], mate)
-            started.append(others[slot])
+        block = fall.at[slot, core, half * 128 : half * 128 + 128]
+        others[slot, half] = send(block, block, cs.at[slot, half], cr.at[slot, half], mate)
+        started.append(others[slot, half])
 
     def arrive(number):
         for way in range(2):
@@ -330,7 +367,8 @@
                     p1[piece, mat, xx, side, yy * 16 : yy * 16 + 16] = rows
 
     def landed(slot):
-        others[slot].wait_recv()
+        for part in range(4):
+            others[slot, part].wait_recv()
 
     def stage(number, piece):
         slot = ORDER[piece]
@@ -467,7 +505,8 @@
             V((64, 256), BF),
             V((256, 256), BF),
             V((64, 128), F32),
-            V((128, 128), F32),
+            V((2, 128, 128), F32),
+            V((2, 2, 64, 256), BF),
             V((512, 256), F32),
             V((512, 256), F32),
             V((512, 256), F32),
@@ -490,8 +529,8 @@
             dma((10,)),
             dma((5,)),
             dma((5,)),
-            dma,
-            dma,
+            dma((2,)),
+            dma((2,)),
             dma((FILTER_DEG + 1, 2)),
             dma((FILTER_DEG + 1, 2)),
             dma((2, 14)),

time: 83.1 us -> 83 us (level)
  no operation moved by 1% of the time
where the time goes in v5:
time: 83 us; the launch traced here: 82.8 us
  Pallas kernels  79.4 us (96%)
  between operations  1.93 us (2%)
  other arithmetic  1.56 us (2%)
    pallas_call x1, Pallas kernels, shards(): pl.pallas_call(kernel, out_shape=(jax.ShapeDtypeStruct((256, 512), F32),...  79.4 us

profile of v5, /device:TPU:2, one launch (start us, length us, event | category | flops | bytes accessed | tf_op | source)
XLA Modules:
  0.0 82.8 jit_solution(4376642124334774101)
XLA Ops:
  1.9 79.4 %shard_map.103 = (f32[256,512]{1,0:T(8,128)S(1)}, f32[16,4096]{1,0:T(8,128)S(1)}, f32[16,4096]{1,0:T(8,128)S(1)}) custom-call(bf16[256,512]{1,0:T(8,128)(2,1)} %x_hbm.1, bf16[125,4,125]{2,1,0:T(4,128)(2,1)} %bitcast.4, s32[4,125]{1,0:T(4,128)} %bitcast.5, s32[1,64]{1,0:T(1,128)} %shared_hbm.1, f32[1,256]{1,0:T(1,128)} %bitcast.6, f32[1,256]{1,0:T(1,128)} %bitcast.7, ...), custom_call_target="tpu_custom_call" | custom-call | tf_op jit(solution)/shard_map/pallas_call | solution.py:470
  81.3 0.7 convert_element_type.3
  82.0 0.8 broadcast_multiply_fusion
